TPU v7x, 256 devices: a whole 4x4x8 slice. The times are simulated.
256 devices in a mesh: seq: 64 (over x, z_lo, y, core), chan: 4 (over z_hi).
Axes of the slice: x: 4, y: 4, z: 8 (z_hi: 4, z_lo: 2; z = z_hi * 2 + z_lo), core: 2. Of those that a mesh axis runs over, the one named last changes fastest.
Arguments:
- layer_input: bfloat16 [16384, 1024], P('seq', 'chan'), may hold values from -6 to 6
- w_in: bfloat16 [1024, 3, 1024], P('seq', None, 'chan'), may hold values from -0.1875 to 0.1875
- filters: float32 [2, 16384, 1024], P(None, 'seq', 'chan'), may hold values from -0.1015625 to 0.1015625, as said below
- bias: float32 [2, 1024], P(None, 'chan'), may hold values from 0.25 to 1.5
- cotangent: bfloat16 [16384, 1024], P('seq', 'chan'), may hold values from -6 to 6
Outputs:
- layer_output: bfloat16 [16384, 1024], P('seq', 'chan')
- grad_u: bfloat16 [16384, 1024], P('seq', 'chan')
- grad_w: float32 [1024, 3, 1024], P('seq', None, 'chan')
- grad_filters: float32 [2, 16384, 1024], P(None, 'seq', 'chan')
- grad_bias: float32 [2, 1024], P(None, 'chan')
Inputs may be any that keep to these rules, and one draw needn't show every extreme that they name: `filters`: each channel of each filter decays exponentially along the lag at a channel-dependent rate.
All inputs are finite; a program needn't handle non-finite values.
Results may differ from a plain program's by a relative error of at most 0.014.
Values may be sent and summed in bfloat16 or wider, within the bound.
A program may use at most 128 MiB of HBM per device.

v0:
```python
import math

import jax
import jax.numpy as jnp
from jax import lax
from jax.sharding import PartitionSpec as P

HIGHEST = lax.Precision.HIGHEST
TWO_PI = 2.0 * math.pi


def rotation(numer, period):
    angle = (numer % period).astype(jnp.float32) * (TWO_PI / period)
    return (jnp.cos(angle), jnp.sin(angle))


def complex_times(left_re, left_im, right_re, right_im):
    return (left_re * right_re - left_im * right_im, left_re * right_im + left_im * right_re)


def on_device(layer_input, w_in, filters, bias, cotangent):
    length, channels = layer_input.shape
    shard_count = lax.axis_size("seq")
    my_index = lax.axis_index("seq")
    period = 2 * shard_count * length
    segment = length // shard_count
    positions = jnp.arange(length, dtype=jnp.int32)
    pair_ids = jnp.arange(2, dtype=jnp.int32)
    cosine, sine = rotation(positions[:, None] * positions[None, :], length)

    def time_dft(real_part, imag_part, sign):
        cos_re = jnp.einsum("st,betc->besc", cosine, real_part, precision=HIGHEST)
        cos_im = jnp.einsum("st,betc->besc", cosine, imag_part, precision=HIGHEST)
        sin_re = jnp.einsum("st,betc->besc", sine, real_part, precision=HIGHEST)
        sin_im = jnp.einsum("st,betc->besc", sine, imag_part, precision=HIGHEST)
        return (cos_re - sign * sin_im, cos_im + sign * sin_re)

    def spectra(signal_in):
        columns = lax.all_to_all(signal_in[:, None], "seq", split_axis=2, concat_axis=1, tiled=True)
        freq_all = jnp.arange(2 * shard_count, dtype=jnp.int32)
        shard_ids = jnp.arange(shard_count, dtype=jnp.int32)
        cos_p, sin_p = rotation(freq_all[:, None] * shard_ids[None, :], 2 * shard_count)
        part_re = jnp.einsum("qp,bptc->bqtc", cos_p, columns, precision=HIGHEST)
        part_im = -jnp.einsum("qp,bptc->bqtc", sin_p, columns, precision=HIGHEST)
        local_pos = my_index * segment + jnp.arange(segment, dtype=jnp.int32)
        tw_cos, tw_sin = rotation(freq_all[:, None] * local_pos[None, :], period)
        tw_cos = tw_cos[None, :, :, None]
        tw_sin = tw_sin[None, :, :, None]
        turned_re = part_re * tw_cos + part_im * tw_sin
        turned_im = part_im * tw_cos - part_re * tw_sin
        rows_re, rows_im = (
            lax.all_to_all(turned_re, "seq", split_axis=1, concat_axis=2, tiled=True),
            lax.all_to_all(turned_im, "seq", split_axis=1, concat_axis=2, tiled=True),
        )
        return time_dft(rows_re, rows_im, -1.0)

    def signal(spec_re, spec_im):
        time_re, time_im = time_dft(spec_re, spec_im, 1.0)
        freq_mine = 2 * my_index + pair_ids
        tw_cos, tw_sin = rotation(freq_mine[:, None] * positions[None, :], period)
        tw_cos = tw_cos[None, :, :, None]
        tw_sin = tw_sin[None, :, :, None]
        turned_re = time_re * tw_cos - time_im * tw_sin
        turned_im = time_im * tw_cos + time_re * tw_sin
        cols_re, cols_im = (
            lax.all_to_all(
                turned_re.astype(jnp.bfloat16), "seq", split_axis=2, concat_axis=1, tiled=True
            ).astype(turned_re.dtype),
            lax.all_to_all(
                turned_im.astype(jnp.bfloat16), "seq", split_axis=2, concat_axis=1, tiled=True
            ).astype(turned_im.dtype),
        )
        freq_all = jnp.arange(2 * shard_count, dtype=jnp.int32)
        shard_ids = jnp.arange(shard_count, dtype=jnp.int32)
        cos_p, sin_p = rotation(shard_ids[:, None] * freq_all[None, :], 2 * shard_count)
        values = (
            jnp.einsum("pq,bqtc->bptc", cos_p, cols_re, precision=HIGHEST)
            - jnp.einsum("pq,bqtc->bptc", sin_p, cols_im, precision=HIGHEST)
        ) / period
        returned = lax.all_to_all(values, "seq", split_axis=1, concat_axis=2, tiled=True)
        return returned[:, 0]

    full_input = lax.all_gather(layer_input, "chan", axis=1, tiled=True)
    flat_cols = 3 * channels
    piece = lax.all_gather(w_in, "seq", axis=0, tiled=True)
    columns = full_input
    proj = jnp.dot(
        columns, piece.reshape(piece.shape[0], flat_cols), preferred_element_type=jnp.float32
    )
    proj = proj.reshape(length, 3, channels)
    values_v = proj[:, 0]
    gate_one = proj[:, 1]
    gate_two = proj[:, 2]
    first_re, first_im = spectra(jnp.stack([filters[0], filters[1], values_v]))
    prod_re, prod_im = complex_times(first_re[0], first_im[0], first_re[2], first_im[2])
    conv_one = signal(prod_re[None], prod_im[None])[0] + bias[0] * values_v
    mixed_one = gate_one * conv_one
    mixed_re, mixed_im = spectra(mixed_one[None])
    prod_re, prod_im = complex_times(first_re[1], first_im[1], mixed_re[0], mixed_im[0])
    conv_two = signal(prod_re[None], prod_im[None])[0] + bias[1] * mixed_one
    output = (gate_two * conv_two).astype(jnp.bfloat16)
    grad_out = cotangent.astype(jnp.float32)
    grad_gate_two = grad_out * conv_two
    grad_conv_two = grad_out * gate_two
    g_two_re, g_two_im = spectra(grad_conv_two[None])
    back_re, back_im = complex_times(first_re[1], -first_im[1], g_two_re[0], g_two_im[0])
    filt_re, filt_im = complex_times(g_two_re[0], g_two_im[0], mixed_re[0], -mixed_im[0])
    second_back = signal(jnp.stack([back_re, filt_re]), jnp.stack([back_im, filt_im]))
    grad_mixed = second_back[0] + bias[1] * grad_conv_two
    grad_filt_two = second_back[1]
    bias_grad_two = jnp.sum(grad_conv_two * mixed_one, axis=0)
    bias_grad_two = lax.psum(bias_grad_two, "seq")
    grad_gate_one = grad_mixed * conv_one
    grad_conv_one = grad_mixed * gate_one
    g_one_re, g_one_im = spectra(grad_conv_one[None])
    back_re, back_im = complex_times(first_re[0], -first_im[0], g_one_re[0], g_one_im[0])
    filt_re, filt_im = complex_times(g_one_re[0], g_one_im[0], first_re[2], -first_im[2])
    first_back = signal(jnp.stack([back_re, filt_re]), jnp.stack([back_im, filt_im]))
    grad_values = first_back[0] + bias[0] * grad_conv_one
    grad_filt_one = first_back[1]
    bias_grad_one = jnp.sum(grad_conv_one * values_v, axis=0)
    bias_grad_one = lax.psum(bias_grad_one, "seq")
    grad_proj = jnp.stack([grad_values, grad_gate_one, grad_gate_two], axis=1).astype(jnp.bfloat16)
    grad_flat = grad_proj.reshape(length, flat_cols)
    piece = lax.all_gather(w_in, "seq", axis=0, tiled=True)
    partial_input = lax.dot_general(
        grad_flat,
        piece.reshape(piece.shape[0], flat_cols),
        (((1,), (1,)), ((), ())),
        preferred_element_type=jnp.float32,
    )
    grad_input = lax.psum_scatter(
        partial_input.astype(jnp.bfloat16), "chan", scatter_dimension=1, tiled=True
    )
    row_count = w_in.shape[0]
    grad_weight = lax.psum_scatter(
        lax.dot_general(
            full_input, grad_flat, (((0,), (0,)), ((), ())), preferred_element_type=jnp.float32
        ),
        "seq",
        scatter_dimension=0,
        tiled=True,
    ).reshape(row_count, 3, channels)
    grad_filt = jnp.stack([grad_filt_one, grad_filt_two])
    grad_skip = jnp.stack([bias_grad_one, bias_grad_two])
    return (output, grad_input, grad_weight, grad_filt, grad_skip)


def solution(mesh):
    in_specs = (
        P("seq", "chan"),
        P("seq", None, "chan"),
        P(None, "seq", "chan"),
        P(None, "chan"),
        P("seq", "chan"),
    )
    out_specs = (
        P("seq", "chan"),
        P("seq", "chan"),
        P("seq", None, "chan"),
        P(None, "seq", "chan"),
        P(None, "chan"),
    )
    return jax.shard_map(
        on_device, mesh=mesh, in_specs=in_specs, out_specs=out_specs, check_vma=False
    )
```

profile of v0, /device:TPU:1, one launch (start us, length us, event | category | flops | bytes accessed | tf_op | source)
XLA Modules:
  0.0 966.5 jit_solution(3091375509386805842)
XLA Ops:
  8.9 18.3 %all_gather.7 = bf16[256,1024]{1,0:T(8,128)(2,1)S(1)} all-gather(bf16[256,256]{1,0:T(8,128)(2,1)} %param.5), channel_id=1, replica_groups=mesh['seq'=64,'chan'=4] {'chan'}, dimensions={1}, use_global_device_ids=true | all-gather | bytes 655360 | tf_op jit(solution)/shard_map/all_gather | solution.py:83
  27.2 92.1 %all-gather.2.cloned.1.call-done = bf16[1024,3,256]{2,0,1:T(8,128)(2,1)} async-done(((bf16[16,3,256]{2,0,1:T(8,128)(2,1)}), bf16[1024,3,256]{2,0,1:T(8,128)(2,1)}) %all-gather.2.cloned.1.call-update) | async-done | bytes 1572880 | tf_op jit(solution)/shard_map/all_gather | solution.py:85
  122.5 6.0 all-to-all-start.12
  130.4 7.9 all-to-all-done.12
  148.6 9.4 all-to-all-done
  163.7 11.4 %all-to-all-done.13 = f32[1,128,4,256]{3,2,0,1:T(4,128)S(1)} async-done(((f32[1,128,4,256]{3,2,0,1:T(4,128)}), f32[1,128,4,256]{3,2,0,1:T(4,128)S(1)}, u32[]{:S(2)}, u32[]{:S(2)}) %all-to-all-start.13) | async-done | bytes 524320 | tf_op jit(solution)/shard_map/all_to_all | solution.py:52
  175.2 5.8 all-to-all-start.14
  193.3 5.7 all-to-all-start.1
  201.6 20.8 %all-to-all-done.1 = f32[3,128,4,256]{3,2,0,1:T(4,128)S(1)} async-done(((f32[3,128,4,256]{3,2,0,1:T(4,128)}), f32[3,128,4,256]{3,2,0,1:T(4,128)S(1)}, u32[]{:S(2)}, u32[]{:S(2)}) %all-to-all-start.1) | async-done | bytes 1572896 | tf_op jit(solution)/shard_map/all_to_all | solution.py:52
  222.4 5.8 all-to-all-start.2
  277.9 7.0 all-to-all-start.4
  285.9 8.9 all-to-all-done.4
  301.3 7.9 all-to-all-done.3
  320.3 8.5 all-to-all-done.5
  334.2 14.4 %all_to_all.333 = f32[1,1,256,256]{3,1,0,2:T(1,128)S(1)} all-to-all(f32[1,1,256,256]{3,1,0,2:T(1,128)} %copy.308), channel_id=1, replica_groups=mesh['seq'=64,'chan'=4] {'seq'}, dimensions={2} | all-to-all | bytes 524288 | tf_op jit(solution)/shard_map/all_to_all | solution.py:39
  362.5 11.5 %all-to-all-done.8 = f32[1,128,4,256]{3,2,0,1:T(4,128)} async-done(((f32[1,128,4,256]{3,2,0,1:T(4,128)}), f32[1,128,4,256]{3,2,0,1:T(4,128)}, u32[]{:S(2)}, u32[]{:S(2)}) %all-to-all-start.8) | async-done | bytes 524320 | tf_op jit(solution)/shard_map/all_to_all | solution.py:53
  415.6 11.2 %all-to-all-done.16 = bf16[2,2,256,256]{3,1,0,2:T(2,128)(2,1)S(1)} async-done(((bf16[2,2,256,256]{3,1,0,2:T(2,128)(2,1)}), bf16[2,2,256,256]{3,1,0,2:T(2,128)(2,1)S(1)}, u32[]{:S(2)}, u32[]{:S(2)}) %all-to-all-start.16) | async-done | bytes 524320 | tf_op jit(solution)/shard_map/all_to_all | solution.py:69
  432.1 11.9 %all-to-all-done.15 = bf16[2,2,256,256]{3,1,0,2:T(2,128)(2,1)S(1)} async-done(((bf16[2,2,256,256]{3,1,0,2:T(2,128)(2,1)}), bf16[2,2,256,256]{3,1,0,2:T(2,128)(2,1)S(1)}, u32[]{:S(2)}, u32[]{:S(2)}) %all-to-all-start.15) | async-done | bytes 524320 | tf_op jit(solution)/shard_map/all_to_all | solution.py:66
  453.4 12.2 %all-to-all-done.17 = f32[2,64,4,256]{3,2,0,1:T(4,128)S(1)} async-done(((f32[2,64,4,256]{3,2,0,1:T(4,128)}), f32[2,64,4,256]{3,2,0,1:T(4,128)S(1)}, u32[]{:S(2)}, u32[]{:S(2)}) %all-to-all-start.17) | async-done | bytes 524320 | tf_op jit(solution)/shard_map/all_to_all | solution.py:80
  468.2 14.3 %all_to_all.334 = f32[1,1,256,256]{3,1,0,2:T(1,128)S(1)} all-to-all(f32[1,1,256,256]{3,1,0,2:T(1,128)S(1)} %copy.346), channel_id=1, replica_groups=mesh['seq'=64,'chan'=4] {'seq'}, dimensions={2} | all-to-all | bytes 524288 | tf_op jit(solution)/shard_map/all_to_all | solution.py:39
  491.9 11.5 %all-to-all-done.19 = f32[1,128,4,256]{3,2,0,1:T(4,128)S(1)} async-done(((f32[1,128,4,256]{3,2,0,1:T(4,128)}), f32[1,128,4,256]{3,2,0,1:T(4,128)S(1)}, u32[]{:S(2)}, u32[]{:S(2)}) %all-to-all-start.19) | async-done | bytes 524320 | tf_op jit(solution)/shard_map/all_to_all | solution.py:52
  511.1 9.4 all-to-all-done.20
  553.1 7.6 all-to-all-start.9
  570.2 6.0 all-to-all-start.22
  577.4 11.3 %all-to-all-done.22 = bf16[2,2,256,256]{3,1,0,2:T(2,128)(2,1)S(1)} async-done(((bf16[2,2,256,256]{3,1,0,2:T(2,128)(2,1)}), bf16[2,2,256,256]{3,1,0,2:T(2,128)(2,1)S(1)}, u32[]{:S(2)}, u32[]{:S(2)}) %all-to-all-start.22) | async-done | bytes 524320 | tf_op jit(solution)/shard_map/all_to_all | solution.py:69
  597.5 8.3 all-to-all-done.21
  605.8 5.3 all-to-all-start.11
  614.4 6.5 all-to-all-done.11
  627.1 11.1 %all-to-all-done.23 = f32[2,64,4,256]{3,2,0,1:T(4,128)S(1)} async-done(((f32[2,64,4,256]{3,2,0,1:T(4,128)}), f32[2,64,4,256]{3,2,0,1:T(4,128)S(1)}, u32[]{:S(2)}, u32[]{:S(2)}) %all-to-all-start.23) | async-done | bytes 524320 | tf_op jit(solution)/shard_map/all_to_all | solution.py:80
  648.3 138.3 %all-reduce = (f32[1,256]{1,0:T(1,128)S(1)}, f32[1,256]{1,0:T(1,128)S(1)}) all-reduce(f32[1,256]{1,0:T(1,128)S(1)} %bitcast.494, f32[1,256]{1,0:T(1,128)S(1)} %bitcast.493), channel_id=1, replica_groups=mesh['seq'=64,'chan'=4] {'seq'}, use_global_device_ids=true, to_apply=%region_5.6 | all-reduce | flops 512 | bytes 4096 | tf_op jit(solution)/shard_map/psum | solution.py:112
  789.6 139.1 %reduce-scatter.7.cloned.1.call-done = f32[16,768]{1,0:T(8,128)} async-done(((f32[1024,768]{1,0:T(8,128)}), f32[16,768]{1,0:T(8,128)}) %reduce-scatter.7.cloned.1.call-update) | async-done | bytes 49168
  930.5 29.3 %reduce-scatter.5.cloned.1.call-done = bf16[256,256]{1,0:T(8,128)(2,1)} async-done(((bf16[256,1024]{1,0:T(8,128)(2,1)}), bf16[256,256]{1,0:T(8,128)(2,1)}) %reduce-scatter.5.cloned.1.call-update) | async-done | bytes 131088 | tf_op jit(solution)/shard_map/reduce_scatter | solution.py:132
  (257 shorter events, 276.4 us)
Async XLA Ops:
  7.2 112.1 %all-gather.2.cloned.1.call-start = ((), (), s32[]{:S(2)}) async-start(), calls=%async_computation.26 | async-start | bytes 1597440 | tf_op jit(solution)/shard_map/all_gather | solution.py:85
  122.5 15.8 %all-to-all-start.12 = ((f32[1,1,256,256]{3,1,0,2:T(1,128)}), f32[1,1,256,256]{3,1,0,2:T(1,128)S(1)}, u32[]{:S(2)}, u32[]{:S(2)}) async-start(f32[1,1,256,256]{3,1,0,2:T(1,128)} %copy.327), calls=%async_computation.12 | async-start | bytes 524288 | tf_op jit(solution)/shard_map/all_to_all | solution.py:39
  138.3 19.8 %all-to-all-start = ((f32[3,1,256,256]{3,1,0,2:T(1,128)}), f32[3,1,256,256]{3,1,0,2:T(1,128)S(1)}, u32[]{:S(2)}, u32[]{:S(2)}) async-start(f32[3,1,256,256]{3,1,0,2:T(1,128)} %copy.288), calls=%async_computation | async-start | bytes 1572864 | tf_op jit(solution)/shard_map/all_to_all | solution.py:39
  158.1 17.1 %all-to-all-start.13 = ((f32[1,128,4,256]{3,2,0,1:T(4,128)}), f32[1,128,4,256]{3,2,0,1:T(4,128)S(1)}, u32[]{:S(2)}, u32[]{:S(2)}) async-start(f32[1,128,4,256]{3,2,0,1:T(4,128)} %copy.330), calls=%async_computation.13 | async-start | bytes 1048576 | tf_op jit(solution)/shard_map/all_to_all | solution.py:52
  175.2 18.1 %all-to-all-start.14 = ((f32[1,128,4,256]{3,2,0,1:T(4,128)}), f32[1,128,4,256]{3,2,0,1:T(4,128)}, u32[]{:S(2)}, u32[]{:S(2)}) async-start(f32[1,128,4,256]{3,2,0,1:T(4,128)} %copy.333), calls=%async_computation.14 | async-start | bytes 1048576 | tf_op jit(solution)/shard_map/all_to_all | solution.py:53
  193.3 29.1 %all-to-all-start.1 = ((f32[3,128,4,256]{3,2,0,1:T(4,128)}), f32[3,128,4,256]{3,2,0,1:T(4,128)S(1)}, u32[]{:S(2)}, u32[]{:S(2)}) async-start(f32[3,128,4,256]{3,2,0,1:T(4,128)} %copy.292), calls=%async_computation.1 | async-start | bytes 3145728 | tf_op jit(solution)/shard_map/all_to_all | solution.py:52
  222.4 29.1 %all-to-all-start.2 = ((f32[3,128,4,256]{3,2,0,1:T(4,128)}), f32[3,128,4,256]{3,2,0,1:T(4,128)}, u32[]{:S(2)}, u32[]{:S(2)}) async-start(f32[3,128,4,256]{3,2,0,1:T(4,128)} %copy.296), calls=%async_computation.2 | async-start | bytes 3145728 | tf_op jit(solution)/shard_map/all_to_all | solution.py:53
  277.9 16.9 %all-to-all-start.4 = ((bf16[1,2,256,256]{3,1,0,2:T(2,128)(2,1)}), bf16[1,2,256,256]{3,1,0,2:T(2,128)(2,1)S(1)}, u32[]{:S(2)}, u32[]{:S(2)}) async-start(bf16[1,2,256,256]{3,1,0,2:T(2,128)(2,1)} %copy.304), calls=%async_computation.4 | async-start | bytes 524288 | tf_op jit(solution)/shard_map/all_to_all | solution.py:69
  294.8 14.4 %all-to-all-start.3 = ((bf16[1,2,256,256]{3,1,0,2:T(2,128)(2,1)}), bf16[1,2,256,256]{3,1,0,2:T(2,128)(2,1)S(1)}, u32[]{:S(2)}, u32[]{:S(2)}) async-start(bf16[1,2,256,256]{3,1,0,2:T(2,128)(2,1)} %copy.302), calls=%async_computation.3 | async-start | bytes 524288 | tf_op jit(solution)/shard_map/all_to_all | solution.py:66
  314.5 14.4 %all-to-all-start.5 = ((f32[1,64,4,256]{3,2,0,1:T(4,128)}), f32[1,64,4,256]{3,2,0,1:T(4,128)S(1)}, u32[]{:S(2)}, u32[]{:S(2)}) async-start(f32[1,64,4,256]{3,2,0,1:T(4,128)} %copy.306), calls=%async_computation.5 | async-start | bytes 524288 | tf_op jit(solution)/shard_map/all_to_all | solution.py:80
  328.8 19.8 %copy-start.12 = (f32[1,64,4,256]{3,2,0,1:T(4,128)}, f32[1,64,4,256]{3,2,0,1:T(4,128)S(1)}, u32[]{:S(2)}) copy-start(f32[1,64,4,256]{3,2,0,1:T(4,128)S(1)} %all-to-all-done.5) | copy-start | bytes 786436
  356.2 17.7 %all-to-all-start.8 = ((f32[1,128,4,256]{3,2,0,1:T(4,128)}), f32[1,128,4,256]{3,2,0,1:T(4,128)}, u32[]{:S(2)}, u32[]{:S(2)}) async-start(f32[1,128,4,256]{3,2,0,1:T(4,128)} %copy.314), calls=%async_computation.8 | async-start | bytes 1048576 | tf_op jit(solution)/shard_map/all_to_all | solution.py:53
  374.0 17.1 %all-to-all-start.7 = ((f32[1,128,4,256]{3,2,0,1:T(4,128)}), f32[1,128,4,256]{3,2,0,1:T(4,128)S(1)}, u32[]{:S(2)}, u32[]{:S(2)}) async-start(f32[1,128,4,256]{3,2,0,1:T(4,128)} %copy.311), calls=%async_computation.7 | async-start | bytes 1048576 | tf_op jit(solution)/shard_map/all_to_all | solution.py:52
  409.7 17.1 %all-to-all-start.16 = ((bf16[2,2,256,256]{3,1,0,2:T(2,128)(2,1)}), bf16[2,2,256,256]{3,1,0,2:T(2,128)(2,1)S(1)}, u32[]{:S(2)}, u32[]{:S(2)}) async-start(bf16[2,2,256,256]{3,1,0,2:T(2,128)(2,1)} %copy.341), calls=%async_computation.16 | async-start | bytes 1048576 | tf_op jit(solution)/shard_map/all_to_all | solution.py:69
  426.8 17.1 %all-to-all-start.15 = ((bf16[2,2,256,256]{3,1,0,2:T(2,128)(2,1)}), bf16[2,2,256,256]{3,1,0,2:T(2,128)(2,1)S(1)}, u32[]{:S(2)}, u32[]{:S(2)}) async-start(bf16[2,2,256,256]{3,1,0,2:T(2,128)(2,1)} %copy.338), calls=%async_computation.15 | async-start | bytes 1048576 | tf_op jit(solution)/shard_map/all_to_all | solution.py:66
  448.5 17.1 %all-to-all-start.17 = ((f32[2,64,4,256]{3,2,0,1:T(4,128)}), f32[2,64,4,256]{3,2,0,1:T(4,128)S(1)}, u32[]{:S(2)}, u32[]{:S(2)}) async-start(f32[2,64,4,256]{3,2,0,1:T(4,128)} %copy.344), calls=%async_computation.17 | async-start | bytes 1048576 | tf_op jit(solution)/shard_map/all_to_all | solution.py:80
  466.6 16.5 %copy-start.10 = (f32[256,256]{0,1:T(8,128)}, f32[256,256]{0,1:T(8,128)S(1)}, u32[]{:S(2)}) copy-start(f32[256,256]{0,1:T(8,128)S(1)} %copy.345) | copy-start | bytes 786436
  468.1 17.3 %copy-start.8 = (f32[256,256]{0,1:T(8,128)}, f32[256,256]{0,1:T(8,128)S(1)}, u32[]{:S(2)}) copy-start(f32[256,256]{0,1:T(8,128)S(1)} %get-tuple-element.34) | copy-start | bytes 786436
  486.4 17.0 %all-to-all-start.19 = ((f32[1,128,4,256]{3,2,0,1:T(4,128)}), f32[1,128,4,256]{3,2,0,1:T(4,128)S(1)}, u32[]{:S(2)}, u32[]{:S(2)}) async-start(f32[1,128,4,256]{3,2,0,1:T(4,128)} %copy.349), calls=%async_computation.19 | async-start | bytes 1048576 | tf_op jit(solution)/shard_map/all_to_all | solution.py:52
  503.4 17.1 %all-to-all-start.20 = ((f32[1,128,4,256]{3,2,0,1:T(4,128)}), f32[1,128,4,256]{3,2,0,1:T(4,128)S(1)}, u32[]{:S(2)}, u32[]{:S(2)}) async-start(f32[1,128,4,256]{3,2,0,1:T(4,128)} %copy.352), calls=%async_computation.20 | async-start | bytes 1048576 | tf_op jit(solution)/shard_map/all_to_all | solution.py:53
  538.0 15.1 %all-to-all-start.10 = ((bf16[1,2,256,256]{3,1,0,2:T(2,128)(2,1)}), bf16[1,2,256,256]{3,1,0,2:T(2,128)(2,1)}, u32[]{:S(2)}, u32[]{:S(2)}) async-start(bf16[1,2,256,256]{3,1,0,2:T(2,128)(2,1)} %copy.321), calls=%async_computation.10 | async-start | bytes 524288 | tf_op jit(solution)/shard_map/all_to_all | solution.py:69
  553.1 17.2 %all-to-all-start.9 = ((bf16[1,2,256,256]{3,1,0,2:T(2,128)(2,1)}), bf16[1,2,256,256]{3,1,0,2:T(2,128)(2,1)}, u32[]{:S(2)}, u32[]{:S(2)}) async-start(bf16[1,2,256,256]{3,1,0,2:T(2,128)(2,1)} %copy.319), calls=%async_computation.9 | async-start | bytes 524288 | tf_op jit(solution)/shard_map/all_to_all | solution.py:66
  570.2 18.4 %all-to-all-start.22 = ((bf16[2,2,256,256]{3,1,0,2:T(2,128)(2,1)}), bf16[2,2,256,256]{3,1,0,2:T(2,128)(2,1)S(1)}, u32[]{:S(2)}, u32[]{:S(2)}) async-start(bf16[2,2,256,256]{3,1,0,2:T(2,128)(2,1)} %copy.360), calls=%async_computation.22 | async-start | bytes 1048576 | tf_op jit(solution)/shard_map/all_to_all | solution.py:69
  588.7 17.1 %all-to-all-start.21 = ((bf16[2,2,256,256]{3,1,0,2:T(2,128)(2,1)}), bf16[2,2,256,256]{3,1,0,2:T(2,128)(2,1)S(1)}, u32[]{:S(2)}, u32[]{:S(2)}) async-start(bf16[2,2,256,256]{3,1,0,2:T(2,128)(2,1)} %copy.357), calls=%async_computation.21 | async-start | bytes 1048576 | tf_op jit(solution)/shard_map/all_to_all | solution.py:66
  605.8 15.1 %all-to-all-start.11 = ((f32[1,64,4,256]{3,2,0,1:T(4,128)}), f32[1,64,4,256]{3,2,0,1:T(4,128)}, u32[]{:S(2)}, u32[]{:S(2)}) async-start(f32[1,64,4,256]{3,2,0,1:T(4,128)} %copy.323), calls=%async_computation.11 | async-start | bytes 524288 | tf_op jit(solution)/shard_map/all_to_all | solution.py:80
  613.2 13.6 %copy-start.11 = (f32[256,256]{0,1:T(8,128)S(1)}, f32[256,256]{0,1:T(8,128)}, u32[]{:S(2)}) copy-start(f32[256,256]{0,1:T(8,128)} %copy-done.10) | copy-start | bytes 786436
  613.2 13.6 %copy-start.24 = (f32[256,256]{0,1:T(8,128)S(1)}, f32[256,256]{0,1:T(8,128)}, u32[]{:S(2)}) copy-start(f32[256,256]{0,1:T(8,128)} %get-tuple-element.35) | copy-start | bytes 786436
  613.2 13.6 %copy-start.37 = (f32[1,256]{1,0:T(1,128)S(1)}, f32[1,256]{1,0:T(1,128)}, u32[]{:S(2)}) copy-start(f32[1,256]{1,0:T(1,128)} %get-tuple-element.73) | copy-start | bytes 3076
  620.9 17.2 %all-to-all-start.23 = ((f32[2,64,4,256]{3,2,0,1:T(4,128)}), f32[2,64,4,256]{3,2,0,1:T(4,128)S(1)}, u32[]{:S(2)}, u32[]{:S(2)}) async-start(f32[2,64,4,256]{3,2,0,1:T(4,128)} %copy.363), calls=%async_computation.23 | async-start | bytes 1048576 | tf_op jit(solution)/shard_map/all_to_all | solution.py:80
  625.6 303.2 %reduce-scatter.7.cloned.1.call-start = ((), (), s32[]{:S(2)}) async-start(), calls=%async_computation.28 | async-start | bytes 3194880
  645.1 314.6 %reduce-scatter.5.cloned.1.call-start = ((), (), s32[]{:S(2)}) async-start(), calls=%async_computation.27 | async-start | bytes 655360 | tf_op jit(solution)/shard_map/reduce_scatter | solution.py:132
  647.9 140.1 %copy-start.26 = (f32[1,64,4,256]{3,2,0,1:T(4,128)S(1)}, f32[1,64,4,256]{3,2,0,1:T(4,128)}, u32[]{:S(2)}) copy-start(f32[1,64,4,256]{3,2,0,1:T(4,128)} %get-tuple-element.69) | copy-start | bytes 786436
  (33 other events, 185.3 us)
Sparse Core Ops, SparseCore 0:
  9.9 109.3 all-gather.1
  645.2 283.4 reduce-scatter.6
  932.0 27.7 reduce-scatter.4
where the time goes:
time: 977 us; the launch traced here: 966 us
  waiting for transfers between devices  456 us (47%)
  blocking collectives  185 us (19%)
  starting transfers between devices  115 us (12%)
  matrix products  100 us (10%)
  local copies, waits for them, and re-layouts  86.9 us (9%)
  between operations  15.3 us (2%)
    unnamed x4, waiting for transfers between devices  140 us
    psum x1, blocking collectives, on_device(): bias_grad_two = lax.psum(bias_grad_two, 'seq')  138 us
    all_gather x1, waiting for transfers between devices, on_device(): piece = lax.all_gather(w_in, 'seq', axis=0, tiled=True)  92.1 us
    all_to_all x4, waiting for transfers between devices, spectra(): lax.all_to_all(turned_re, 'seq', split_axis=1, concat_axis=2, tiled=True)  48.5 us
    all_to_all x4, waiting for transfers between devices, signal(): lax.all_to_all(values, 'seq', split_axis=1, concat_axis=2, tiled=True)  38.3 us
    all_to_all x4, waiting for transfers between devices, signal(): lax.all_to_all(turned_im.astype(jnp.bfloat16), 'seq', split_axis=2, conca...  33.6 us
    all_to_all x4, waiting for transfers between devices, signal(): lax.all_to_all(turned_re.astype(jnp.bfloat16), 'seq', split_axis=2, conca...  31 us
    reduce_scatter x1, waiting for transfers between devices, on_device(): lax.psum_scatter(partial_input.astype(jnp.bfloat16), 'chan', scatter_dime...  29.3 us
  transfers between devices with their start and end apart: 25, of which 25 were waited for; matrix products, arithmetic and copies ran while one was open for 9% of the time, Pallas kernels for 0%

commit v1 on v0

v1 whole, which is shorter than its diff:
```python
import functools
import math

import jax
import jax.numpy as jnp
import ml_dtypes
import numpy as np
from jax import lax
from jax.experimental import pallas as pl
from jax.experimental.pallas import tpu as pltpu
from jax.sharding import PartitionSpec as P

MESH = pl.DeviceIdType.MESH
LANES = 128
BF16 = jnp.bfloat16
F32 = jnp.float32


def tables(blocks):
    period = 2 * blocks * LANES
    chips = blocks // 4
    order = np.array([4 * j + tb for tb in range(4) for j in range(chips)])
    freq = np.arange(blocks) + 0.5
    lane = np.arange(LANES)
    angle = 2.0 * math.pi * freq[:, None] * order[None, :] / (2 * blocks)
    first = np.concatenate([np.cos(angle), -np.sin(angle)], axis=0)
    turn = 2.0 * math.pi * freq[:, None] * lane[None, :] / period
    inner = 2.0 * math.pi * ((lane[:, None] * lane[None, :]) % LANES) / LANES
    cosine, sine = np.cos(inner), np.sin(inner)
    middle = np.block([[cosine, -sine], [sine, cosine]])
    last = first.T * (2.0 / period)

    def parts(table, axis):
        high = table.astype(ml_dtypes.bfloat16)
        low = (table - high.astype(np.float64)).astype(ml_dtypes.bfloat16)
        return np.concatenate([high, low, high], axis=axis)

    return (
        parts(first, 1),
        parts(middle, 0),
        parts(middle.T, 0),
        parts(last, 1),
        np.cos(turn).astype(np.float32),
        np.sin(turn).astype(np.float32),
    )


def matmul(left, right, dims=((1,), (0,))):
    return lax.dot_general(left, right, (dims, ((), ())), preferred_element_type=F32)


def split(value):
    high = value.astype(BF16)
    low = (value - high.astype(F32)).astype(BF16)
    return high, low


def greet(me, peers, group, groups):
    barrier = pltpu.get_barrier_semaphore()

    def one(step, carry):
        pl.semaphore_signal(
            barrier, inc=1, device_id=(lax.rem(me + step, peers), group), device_id_type=MESH
        )
        return carry

    lax.fori_loop(1, peers, one, 0)
    for step in range(1, groups):
        pl.semaphore_signal(
            barrier, inc=1, device_id=(me, lax.rem(group + step, groups)), device_id_type=MESH
        )
    return barrier


def wait_bytes(ref, sem):
    pltpu.make_async_copy(ref, ref, sem).wait()


def gather_kernel(
    n, groups, x_ref, w_ref, filters_ref, cot_ref,
    wg_ref, xg_ref, a_recv, b_recv,
    stage_a, a_send, stage_b, b_send, sems, x_sems,
):
    me = lax.axis_index("seq")
    group = lax.axis_index("chan")
    core = lax.rem(me, 2)
    chip = me // 2
    partner = me + 1 - 2 * core
    chips = n // 2
    quota = LANES // chips
    rows_a, rows_b = a_send.shape[1], b_send.shape[1]
    barrier = greet(me, n, group, groups)

    def stage_early(value, base):
        turned = value.T
        for half in range(2):
            for q in range(quota):
                top = half * LANES + q * chips
                for tb in range(2):
                    stage_b[pl.ds(half * rows_b + base + q * 2 + tb, chips, stride=2 * rows_b), :] = turned[
                        top : top + chips, tb * LANES : (tb + 1) * LANES
                    ]

    stage_early(filters_ref[0], 0)
    stage_early(filters_ref[1], 2 * quota)
    stage_early(cot_ref[...].astype(F32), 4 * quota)
    for peer in range(n):
        stage_b[pl.ds(peer * rows_b + 6 * quota, 2 * quota), :] = jnp.zeros((2 * quota, LANES), F32)
    b_send[...] = stage_b[...].astype(BF16).reshape(b_send.shape)
    xg_ref[core, group] = x_ref[...]
    pl.semaphore_wait(barrier, n - 1 + groups - 1)

    def send_w(step, carry):
        peer = lax.rem(me + step, n)
        pltpu.make_async_remote_copy(
            src_ref=w_ref.at[lax.rem(peer, 2)], dst_ref=wg_ref.at[me],
            send_sem=sems.at[0], recv_sem=sems.at[1],
            device_id=(peer, group), device_id_type=MESH,
        ).start()
        return carry

    for step in range(1, groups):
        pltpu.make_async_remote_copy(
            src_ref=x_ref, dst_ref=xg_ref.at[core, group],
            send_sem=sems.at[2], recv_sem=x_sems.at[group],
            device_id=(me, lax.rem(group + step, groups)), device_id_type=MESH,
        ).start()
    lax.fori_loop(1, n, send_w, 0)
    pltpu.make_async_copy(w_ref.at[core], wg_ref.at[me], sems.at[1]).start()
    pltpu.make_async_remote_copy(
        src_ref=x_ref, dst_ref=xg_ref.at[core, group],
        send_sem=sems.at[2], recv_sem=sems.at[3],
        device_id=(partner, group), device_id_type=MESH,
    ).start()

    def send_b(step, carry):
        peer = lax.rem(me + step, n)
        pltpu.make_async_remote_copy(
            src_ref=b_send.at[peer], dst_ref=b_recv.at[me],
            send_sem=sems.at[4], recv_sem=sems.at[5],
            device_id=(peer, group), device_id_type=MESH,
        ).start()
        return carry

    lax.fori_loop(1, n, send_b, 0)
    pltpu.make_async_copy(b_send.at[me], b_recv.at[me], sems.at[5]).start()

    for step in range(1, groups):
        other = lax.rem(group + groups - step, groups)
        wait_bytes(xg_ref.at[core, other], x_sems.at[other])
        pltpu.make_async_remote_copy(
            src_ref=xg_ref.at[core, other], dst_ref=xg_ref.at[core, other],
            send_sem=sems.at[6], recv_sem=sems.at[3],
            device_id=(partner, group), device_id_type=MESH,
        ).start()
    wait_bytes(wg_ref, sems.at[1])
    wait_bytes(xg_ref.at[1 - core], sems.at[3])

    depth = x_ref.shape[1]
    slots = depth // wg_ref.shape[1]
    tokens = x_ref.shape[0]
    total = None
    for c in range(groups):
        rows = xg_ref[:, c].reshape(2 * tokens, depth)
        block = wg_ref[c * slots : (c + 1) * slots].reshape(depth, wg_ref.shape[2])
        term = matmul(rows, block)
        total = term if total is None else total + term
    turned = total.T
    for a in range(3):
        for q in range(quota):
            top = a * LANES + q * chips
            for tb in range(4):
                stage_a[pl.ds((a * quota + q) * 4 + tb, chips, stride=rows_a), :] = turned[
                    top : top + chips, tb * LANES : (tb + 1) * LANES
                ]
    a_send[...] = stage_a[...].astype(BF16).reshape(a_send.shape)

    def send_a(step, carry):
        peer = lax.rem(chip + step, chips)
        pltpu.make_async_remote_copy(
            src_ref=a_send.at[peer], dst_ref=a_recv.at[chip],
            send_sem=sems.at[7], recv_sem=sems.at[8],
            device_id=(2 * peer + core, group), device_id_type=MESH,
        ).start()
        return carry

    lax.fori_loop(1, chips, send_a, 0)
    pltpu.make_async_copy(a_send.at[chip], a_recv.at[chip], sems.at[8]).start()

    wait_bytes(wg_ref.at[pl.ds(0, n - 1)], sems.at[0])
    wait_bytes(xg_ref.at[0], sems.at[2])
    if groups > 1:
        wait_bytes(xg_ref.at[0, pl.ds(0, groups - 1)], sems.at[6])
    wait_bytes(b_recv.at[pl.ds(0, n - 1)], sems.at[4])
    wait_bytes(a_recv.at[pl.ds(0, chips - 1)], sems.at[7])
    wait_bytes(b_recv, sems.at[5])
    wait_bytes(a_recv, sems.at[8])


def conv_kernel(
    n, a_recv, b_recv, bias_ref, first_ref, middle_ref, middle_t_ref, last_ref, cos_ref, sin_ref,
    a_send, b_send,
    stage_a, stage_b, spec_h1, spec_h2, spec_v, spec_z, spec_g,
):
    me = lax.axis_index("seq")
    core = lax.rem(me, 2)
    chip = me // 2
    chips = n // 2
    quota = LANES // chips
    blocks = 4 * chips
    rows_a, rows_b = a_recv.shape[1], b_recv.shape[1]
    stage_a[...] = a_recv[...].reshape(stage_a.shape).astype(F32)
    stage_b[...] = b_recv[...].reshape(stage_b.shape).astype(F32)

    def columns(start, stride):
        return jnp.concatenate(
            [
                jnp.concatenate(
                    [start(q, tb)[0][pl.ds(start(q, tb)[1], chips, stride=stride), :] for q in range(quota)],
                    axis=1,
                )
                for tb in range(4)
            ],
            axis=0,
        )

    def late(a):
        return columns(lambda q, tb: (stage_a, (a * quota + q) * 4 + tb), rows_a)

    def early(base):
        return columns(lambda q, tb: (stage_b, (tb // 2) * rows_b + base + q * 2 + tb % 2), 2 * rows_b)

    def piece(value, q):
        return value[:, q * LANES : (q + 1) * LANES]

    def forward(value, spec, exact=False):
        high, low = split(value)
        if exact:
            wide = matmul(first_ref[:, : 2 * blocks], jnp.concatenate([high, high], axis=0))
        else:
            wide = matmul(first_ref[...], jnp.concatenate([high, high, low], axis=0))
        turn_cos, turn_sin = cos_ref[...], sin_ref[...]
        for q in range(quota):
            re = piece(wide[:blocks], q)
            im = piece(wide[blocks:], q)
            high, low = split(
                jnp.concatenate([re * turn_cos + im * turn_sin, im * turn_cos - re * turn_sin], axis=1)
            )
            spec[q * blocks : (q + 1) * blocks, :] = matmul(
                jnp.concatenate([high, high, low], axis=1), middle_ref[...]
            )

    def backward(left, right, conj_left, conj_right):
        turn_cos, turn_sin = cos_ref[...], sin_ref[...]
        columns_high, columns_low = [], []
        for q in range(quota):
            rows = slice(q * blocks, (q + 1) * blocks)
            l_re, l_im = left[rows, :LANES], left[rows, LANES:]
            r_re, r_im = right[rows, :LANES], right[rows, LANES:]
            cross = l_im * r_im
            y_re = l_re * r_re - (cross if conj_left == conj_right else -cross)
            if conj_left:
                y_im = l_re * r_im - l_im * r_re
            elif conj_right:
                y_im = l_im * r_re - l_re * r_im
            else:
                y_im = l_re * r_im + l_im * r_re
            high, low = split(jnp.concatenate([y_re, y_im], axis=1))
            out = matmul(jnp.concatenate([high, high, low], axis=1), middle_t_ref[...])
            re, im = out[:, :LANES], out[:, LANES:]
            high, low = split(
                jnp.concatenate([re * turn_cos - im * turn_sin, im * turn_cos + re * turn_sin], axis=0)
            )
            columns_high.append(high)
            columns_low.append(low)
        high = jnp.concatenate(columns_high, axis=1)
        low = jnp.concatenate(columns_low, axis=1)
        return matmul(last_ref[...], jnp.concatenate([high, high, low], axis=0))

    def skip(f):
        return jnp.concatenate(
            [
                jnp.full((1, LANES), bias_ref[f, core * LANES + q * chips + chip], F32)
                for q in range(quota)
            ],
            axis=1,
        )

    def store_late(value, a):
        for q in range(quota):
            for tb in range(4):
                stage_a[pl.ds((a * quota + q) * 4 + tb, chips, stride=rows_a), :] = piece(value, q)[
                    tb * chips : (tb + 1) * chips
                ]

    def store_early(value, base):
        for q in range(quota):
            for tb in range(4):
                at = (tb // 2) * rows_b + base + q * 2 + tb % 2
                stage_b[pl.ds(at, chips, stride=2 * rows_b), :] = piece(value, q)[
                    tb * chips : (tb + 1) * chips
                ]

    def store_skip(product, f):
        lane = lax.broadcasted_iota(jnp.int32, (1, LANES), 1)
        sums = jnp.sum(product, axis=0, keepdims=True)
        for q in range(quota):
            value = jnp.sum(piece(sums, q), axis=1, keepdims=True)
            one = value.astype(BF16).astype(F32)
            two = (value - one).astype(BF16).astype(F32)
            three = value - one - two
            row = jnp.where(lane == chip, one, 0.0)
            row = jnp.where(lane == chips + chip, two, row)
            row = jnp.where(lane == 2 * chips + chip, three, row)
            for half in range(2):
                at = half * rows_b + 6 * quota + f * quota + q
                stage_b[pl.ds(at, chips, stride=2 * rows_b), :] = jnp.broadcast_to(row, (chips, LANES))

    values_v, gate_one, gate_two = late(0), late(1), late(2)
    forward(early(0), spec_h1, True)
    forward(early(2 * quota), spec_h2, True)
    grad_out = early(4 * quota)
    skip_one, skip_two = skip(0), skip(1)
    forward(values_v, spec_v, True)
    conv_one = backward(spec_h1, spec_v, False, False) + skip_one * values_v
    mixed = gate_one * conv_one
    forward(mixed, spec_z)
    conv_two = backward(spec_h2, spec_z, False, False) + skip_two * mixed
    store_early(gate_two * conv_two, 4 * quota)
    store_late(grad_out * conv_two, 2)
    grad_conv_two = grad_out * gate_two
    forward(grad_conv_two, spec_g)
    store_skip(grad_conv_two * mixed, 1)
    grad_mixed = backward(spec_h2, spec_g, True, False) + skip_two * grad_conv_two
    store_early(backward(spec_g, spec_z, False, True), 2 * quota)
    store_late(grad_mixed * conv_one, 1)
    grad_conv_one = grad_mixed * gate_one
    forward(grad_conv_one, spec_g)
    store_skip(grad_conv_one * values_v, 0)
    store_late(backward(spec_h1, spec_g, True, False) + skip_one * grad_conv_one, 0)
    store_early(backward(spec_g, spec_v, False, True), 0)
    a_send[...] = stage_a[...].astype(BF16).reshape(a_send.shape)
    b_send[...] = stage_b[...].astype(BF16).reshape(b_send.shape)


def return_kernel(
    n, groups, a_send, b_send, xg_ref, wg_ref,
    out_ref, gu_ref, gw_ref, gf_ref, gb_ref,
    a_recv, b_recv, stage_a, stage_b, turned_ref, grad_ref, u_own, u_part, u_in, u_send, u_recv,
    w_send, w_recv, sems, u_sems,
):
    me = lax.axis_index("seq")
    group = lax.axis_index("chan")
    core = lax.rem(me, 2)
    chip = me // 2
    partner = me + 1 - 2 * core
    chips = n // 2
    quota = LANES // chips
    rows_a, rows_b = a_send.shape[1], b_send.shape[1]
    barrier = greet(me, n, group, groups)
    pl.semaphore_wait(barrier, n - 1 + groups - 1)

    def send_a(step, carry):
        peer = lax.rem(chip + step, chips)
        pltpu.make_async_remote_copy(
            src_ref=a_send.at[peer], dst_ref=a_recv.at[chip],
            send_sem=sems.at[0], recv_sem=sems.at[1],
            device_id=(2 * peer + core, group), device_id_type=MESH,
        ).start()
        return carry

    def send_b(step, carry):
        peer = lax.rem(me + step, n)
        pltpu.make_async_remote_copy(
            src_ref=b_send.at[peer], dst_ref=b_recv.at[me],
            send_sem=sems.at[2], recv_sem=sems.at[3],
            device_id=(peer, group), device_id_type=MESH,
        ).start()
        return carry

    lax.fori_loop(1, chips, send_a, 0)
    pltpu.make_async_copy(a_send.at[chip], a_recv.at[chip], sems.at[1]).start()
    lax.fori_loop(1, n, send_b, 0)
    pltpu.make_async_copy(b_send.at[me], b_recv.at[me], sems.at[3]).start()

    wait_bytes(a_recv, sems.at[1])
    stage_a[...] = a_recv[...].reshape(stage_a.shape).astype(F32)
    for a in range(3):
        for q in range(quota):
            top = a * LANES + q * chips
            for tb in range(4):
                turned_ref[top : top + chips, tb * LANES : (tb + 1) * LANES] = stage_a[
                    pl.ds((a * quota + q) * 4 + tb, chips, stride=rows_a), :
                ]
    tokens, depth = xg_ref.shape[2], xg_ref.shape[3]
    grad = turned_ref[...].T.astype(BF16)
    grad_ref[...] = grad.reshape(grad_ref.shape)
    slots = depth // wg_ref.shape[1]

    def weights(c):
        return wg_ref[c * slots : (c + 1) * slots].reshape(depth, wg_ref.shape[2])

    theirs = grad_ref[1 - core]
    for c in range(groups):
        u_part[c] = matmul(theirs, weights(c), ((1,), (1,))).astype(BF16)
    pltpu.make_async_remote_copy(
        src_ref=u_part, dst_ref=u_in, send_sem=sems.at[4], recv_sem=sems.at[5],
        device_id=(partner, group), device_id_type=MESH,
    ).start()
    for c in range(groups):
        rows = xg_ref[:, c].reshape(2 * tokens, depth)
        term = matmul(rows, grad, ((0,), (0,))).astype(BF16)
        w_send[c * slots : (c + 1) * slots] = term.reshape(slots, depth // slots, term.shape[1])

    def send_w(step, carry):
        peer = lax.rem(me + step, n)
        pltpu.make_async_remote_copy(
            src_ref=w_send.at[peer], dst_ref=w_recv.at[me],
            send_sem=sems.at[6], recv_sem=sems.at[7],
            device_id=(peer, group), device_id_type=MESH,
        ).start()
        return carry

    lax.fori_loop(1, n, send_w, 0)
    pltpu.make_async_copy(w_send.at[me], w_recv.at[me], sems.at[7]).start()

    mine = grad_ref[core]
    for c in range(groups):
        u_own[c] = matmul(mine, weights(c), ((1,), (1,)))
    wait_bytes(u_in, sems.at[5])
    for c in range(groups):
        both = u_own[c] + u_in[c].astype(F32)
        u_own[c] = both
        u_send[c] = both.astype(BF16)
    for step in range(1, groups):
        other = lax.rem(group + step, groups)
        pltpu.make_async_remote_copy(
            src_ref=u_send.at[other], dst_ref=u_recv.at[group],
            send_sem=sems.at[8], recv_sem=u_sems.at[group],
            device_id=(me, other), device_id_type=MESH,
        ).start()

    wait_bytes(b_recv, sems.at[3])
    stage_b[...] = b_recv[...].reshape(stage_b.shape).astype(F32)

    def collect(base):
        for half in range(2):
            for q in range(quota):
                top = half * LANES + q * chips
                for tb in range(2):
                    turned_ref[top : top + chips, tb * LANES : (tb + 1) * LANES] = stage_b[
                        pl.ds(half * rows_b + base + q * 2 + tb, chips, stride=2 * rows_b), :
                    ]
        return turned_ref[: 2 * LANES, : 2 * LANES].T

    gf_ref[0] = collect(0)
    gf_ref[1] = collect(2 * quota)
    out_ref[...] = collect(4 * quota).astype(BF16)
    lane = lax.broadcasted_iota(jnp.int32, (1, LANES), 1)
    for f in range(2):
        for half in range(2):
            line = jnp.zeros((1, LANES), F32)
            for q in range(quota):
                at = half * rows_b + 6 * quota + f * quota + q
                row = jnp.sum(stage_b[pl.ds(at, chips, stride=2 * rows_b), :], axis=0, keepdims=True)
                full = row + pltpu.roll(row, LANES - chips, 1) + pltpu.roll(row, LANES - 2 * chips, 1)
                moved = full if q == 0 else pltpu.roll(full, q * chips, 1)
                line = jnp.where((lane >= q * chips) & (lane < (q + 1) * chips), moved, line)
            gb_ref[f : f + 1, half * LANES : (half + 1) * LANES] = line

    total = u_own[group]
    for step in range(1, groups):
        other = lax.rem(group + step, groups)
        wait_bytes(u_recv.at[other], u_sems.at[other])
        total = total + u_recv[other].astype(F32)
    gu_ref[...] = total.astype(BF16)

    wait_bytes(w_recv, sems.at[7])
    for half in range(2):
        acc = w_recv[half].astype(F32)
        for j in range(1, chips):
            acc = acc + w_recv[2 * j + half].astype(F32)
        gw_ref[half] = acc

    wait_bytes(a_recv.at[pl.ds(0, chips - 1)], sems.at[0])
    wait_bytes(b_recv.at[pl.ds(0, n - 1)], sems.at[2])
    wait_bytes(u_in, sems.at[4])
    wait_bytes(w_recv.at[pl.ds(0, n - 1)], sems.at[6])
    if groups > 1:
        wait_bytes(u_recv.at[pl.ds(0, groups - 1)], sems.at[8])


def on_device(layer_input, w_in, filters, bias, cotangent):
    n = lax.axis_size("seq")
    groups = lax.axis_size("chan")
    tokens, width = layer_input.shape
    rows = w_in.shape[0]
    chips = n // 2
    quota = LANES // chips
    rows_a, rows_b = 12 * quota, 8 * quota
    cols = 3 * LANES
    vmem = pl.BlockSpec(memory_space=pltpu.VMEM)
    smem = pl.BlockSpec(memory_space=pltpu.SMEM)
    sds = jax.ShapeDtypeStruct
    dma = pltpu.SemaphoreType.DMA
    limit = 60 * 1024 * 1024

    w_halves = w_in.reshape(rows, 3, 2, LANES).transpose(2, 0, 1, 3).reshape(2, rows, cols)
    wg, xg, a_in, b_in = pl.pallas_call(
        functools.partial(gather_kernel, n, groups),
        out_shape=(
            sds((n, rows, cols), BF16),
            sds((2, groups, tokens, width), BF16),
            sds((chips, rows_a, LANES), BF16),
            sds((n, rows_b, LANES), BF16),
        ),
        in_specs=[vmem] * 4,
        out_specs=(vmem,) * 4,
        scratch_shapes=[
            pltpu.VMEM((chips * rows_a, LANES), F32),
            pltpu.VMEM((chips, rows_a, LANES), BF16),
            pltpu.VMEM((n * rows_b, LANES), F32),
            pltpu.VMEM((n, rows_b, LANES), BF16),
            dma((9,)),
            dma((groups,)),
        ],
        compiler_params=pltpu.CompilerParams(
            collective_id=0, has_side_effects=True, vmem_limit_bytes=limit
        ),
        name="gather",
    )(layer_input, w_halves, filters, cotangent)

    blocks = 4 * chips
    spec = pltpu.VMEM((quota * blocks, 2 * LANES), F32)
    a_out, b_out = pl.pallas_call(
        functools.partial(conv_kernel, n),
        out_shape=(sds(a_in.shape, BF16), sds(b_in.shape, BF16)),
        in_specs=[vmem, vmem, smem] + [vmem] * 6,
        out_specs=(vmem, vmem),
        scratch_shapes=[
            pltpu.VMEM((chips * rows_a, LANES), F32),
            pltpu.VMEM((n * rows_b, LANES), F32),
            spec, spec, spec, spec, spec,
        ],
        compiler_params=pltpu.CompilerParams(vmem_limit_bytes=limit),
        name="convolve",
    )(a_in, b_in, bias, *(jnp.asarray(table) for table in tables(blocks)))

    out, grad_u, grad_w, grad_f, grad_b = pl.pallas_call(
        functools.partial(return_kernel, n, groups),
        out_shape=(
            sds((tokens, width), BF16),
            sds((tokens, width), BF16),
            sds((2, rows, cols), F32),
            sds((2, tokens, width), F32),
            sds((2, width), F32),
        ),
        in_specs=[vmem] * 4,
        out_specs=(vmem,) * 5,
        scratch_shapes=[
            pltpu.VMEM((chips, rows_a, LANES), BF16),
            pltpu.VMEM((n, rows_b, LANES), BF16),
            pltpu.VMEM((chips * rows_a, LANES), F32),
            pltpu.VMEM((n * rows_b, LANES), F32),
            pltpu.VMEM((cols, 2 * tokens), F32),
            pltpu.VMEM((2, tokens, cols), BF16),
            pltpu.VMEM((groups, tokens, width), F32),
            pltpu.VMEM((groups, tokens, width), BF16),
            pltpu.VMEM((groups, tokens, width), BF16),
            pltpu.VMEM((groups, tokens, width), BF16),
            pltpu.VMEM((groups, tokens, width), BF16),
            pltpu.VMEM((n, rows, cols), BF16),
            pltpu.VMEM((n, rows, cols), BF16),
            dma((9,)),
            dma((groups,)),
        ],
        compiler_params=pltpu.CompilerParams(
            collective_id=1, has_side_effects=True, vmem_limit_bytes=limit
        ),
        name="give_back",
    )(a_out, b_out, xg, wg)
    grad_w = grad_w.reshape(2, rows, 3, LANES).transpose(1, 2, 0, 3).reshape(rows, 3, width)
    return (out, grad_u, grad_w, grad_f, grad_b)


def solution(mesh):
    in_specs = (
        P("seq", "chan"),
        P("seq", None, "chan"),
        P(None, "seq", "chan"),
        P(None, "chan"),
        P("seq", "chan"),
    )
    out_specs = (
        P("seq", "chan"),
        P("seq", "chan"),
        P("seq", None, "chan"),
        P(None, "seq", "chan"),
        P(None, "chan"),
    )
    return jax.shard_map(
        on_device, mesh=mesh, in_specs=in_specs, out_specs=out_specs, check_vma=False
    )
```

time: 977 us -> 103 us (0.11); the launches traced: 966 us -> 103 us
  waiting for transfers between devices: 456 us -> 0 us
  blocking collectives: 185 us -> 0 us
  starting transfers between devices: 115 us -> 0 us
  matrix products: 100 us -> 0 us
  Pallas kernels: 0 us -> 94.4 us
  local copies, waits for them, and re-layouts: 86.9 us -> 7.5 us
  between operations: 15.3 us -> 0.68 us
    all_to_all x22 -> x0, waiting for transfers between devices: 195 us -> none  [the longest x4 48.5 us: spectra(): lax.all_to_all(turned_re, 'seq', split_axis=1, concat_axis=2, tiled=True)]
    unnamed x4 -> x0, waiting for transfers between devices: 140 us -> none
    psum x1 -> x0, blocking collectives: 138 us -> none  [on_device(): bias_grad_two = lax.psum(bias_grad_two, 'seq')]
    all_to_all x22 -> x0, starting transfers between devices: 115 us -> none  [the longest x4 22.9 us: signal(): lax.all_to_all(turned_im.astype(jnp.bfloat16), 'seq', split_axis=2, conca...]
    dot_general x51 -> x0, matrix products: 100 us -> none  [the longest x8 21.2 us: time_dft(): sin_re = jnp.einsum('st,betc->besc', sine, real_part, precision=HIGHEST)]
    pallas_call x0 -> x3, Pallas kernels: none -> 94.4 us  [the longest x1 44.6 us: on_device(): pl.pallas_call(functools.partial(gather_kernel, n, groups), out_shape=(sd...]
    all_gather x1 -> x0, waiting for transfers between devices: 92.1 us -> none  [on_device(): piece = lax.all_gather(w_in, 'seq', axis=0, tiled=True)]
    reduce_scatter x1 -> x0, waiting for transfers between devices: 29.3 us -> none  [on_device(): lax.psum_scatter(partial_input.astype(jnp.bfloat16), 'chan', scatter_dime...]
  transfers between devices with their start and end apart: 25 -> 0, of which waited for: 25 -> 0; matrix products, arithmetic and copies ran while one was open for 9% -> 0% of each run, Pallas kernels for 0% -> 0%
where the time goes in v1:
time: 103 us
  Pallas kernels  94.4 us (92%)
  local copies, waits for them, and re-layouts  7.5 us (7%)
    pallas_call x1, Pallas kernels, on_device(): pl.pallas_call(functools.partial(gather_kernel, n, groups), out_shape=(sd...  44.6 us
    pallas_call x1, Pallas kernels, on_device(): pl.pallas_call(functools.partial(return_kernel, n, groups), out_shape=(sd...  40.8 us
    pallas_call x1, Pallas kernels, on_device(): pl.pallas_call(functools.partial(conv_kernel, n), out_shape=(sds(a_in.sha...  9 us
    unnamed x8, local copies, waits for them, and re-layouts  4.51 us

profile of v1, /device:TPU:1, one launch (start us, length us, event | category | flops | bytes accessed | tf_op | source)
XLA Modules:
  0.0 102.6 jit_solution(1878308735207091323)
XLA Ops:
  0.6 0.8 reshape.22
  1.4 0.6 reshape.23.w_ref
  2.0 44.6 %gather.1 = (bf16[64,16,384]{2,1,0:T(8,128)(2,1)}, bf16[2,4,256,256]{3,2,1,0:T(8,128)(2,1)}, bf16[32,48,128]{2,1,0:T(8,128)(2,1)}, bf16[64,32,128]{2,1,0:T(8,128)(2,1)}) custom-call(bf16[256,256]{1,0:T(8,128)(2,1)} %x_ref.1, bf16[2,16,384]{2,1,0:T(8,128)(2,1)} %reshape.23.w_ref, f32[2,256,256]{2,1,0:T(8,128)} %filters_ref.1, bf16[256,256]{1,0:T(8,128)(2,1)} %cot_ref.1), custom_call_target="tpu_custom_call" | custom-call | tf_op jit(solution)/shard_map/gather/pallas_call | solution.py:509
  46.7 9.0 %convolve.1 = (bf16[32,48,128]{2,1,0:T(8,128)(2,1)}, bf16[64,32,128]{2,1,0:T(8,128)(2,1)}) custom-call(bf16[32,48,128]{2,1,0:T(8,128)(2,1)} %get-tuple-element.16.a_recv, bf16[64,32,128]{2,1,0:T(8,128)(2,1)} %get-tuple-element.17.b_recv, f32[2,256]{1,0:T(2,128)} %bias_ref.1, bf16[256,384]{1,0:T(8,128)(2,1)} %constant.12.clone.first_ref, ...), custom_call_target="tpu_custom_call" | custom-call | tf_op jit(solution)/shard_map/convolve/pallas_call | solution.py:535
  55.7 40.8 %give_back.1 = (bf16[256,256]{1,0:T(8,128)(2,1)}, bf16[256,256]{1,0:T(8,128)(2,1)}, f32[2,16,384]{2,1,0:T(8,128)}, f32[2,256,256]{2,1,0:T(8,128)}, f32[2,256]{1,0:T(2,128)}) custom-call(bf16[32,48,128]{2,1,0:T(8,128)(2,1)} %get-tuple-element.18.a_send, bf16[64,32,128]{2,1,0:T(8,128)(2,1)} %get-tuple-element.19.b_send, ...), custom_call_target="tpu_custom_call" | custom-call | tf_op jit(solution)/shard_map/give_back/pallas_call | solution.py:549
  96.5 0.0 copy-start
  96.5 0.9 reshape.24
  97.4 0.7 reshape.25
  98.1 1.6 %copy.27 = bf16[256,256]{1,0:T(8,128)(2,1)} copy(bf16[256,256]{1,0:T(8,128)(2,1)} %get-tuple-element.32) | data formatting | bytes 262144
  99.6 1.6 %copy.28 = bf16[256,256]{1,0:T(8,128)(2,1)} copy(bf16[256,256]{1,0:T(8,128)(2,1)} %get-tuple-element.33) | data formatting | bytes 262144
  101.2 0.0 copy-done
  101.2 0.0 copy-start.1
  101.2 0.8 copy.29
  102.0 0.0 copy-done.1
  102.0 0.6 copy.30
  (2 shorter events, 0.1 us)
Async XLA Ops:
  96.5 4.7 %copy-start = (f32[2,256,256]{2,1,0:T(8,128)S(1)}, f32[2,256,256]{2,1,0:T(8,128)}, u32[]{:S(2)}) copy-start(f32[2,256,256]{2,1,0:T(8,128)} %get-tuple-element.35) | copy-start | bytes 1572868
  101.2 0.8 copy-start.1

commit v2 on v1

v2 whole, which is shorter than its diff:
```python
import functools
import math

import jax
import jax.numpy as jnp
import ml_dtypes
import numpy as np
from jax import lax
from jax.experimental import pallas as pl
from jax.experimental.pallas import tpu as pltpu
from jax.sharding import PartitionSpec as P

MESH = pl.DeviceIdType.MESH
LANES = 128
BF16 = jnp.bfloat16
F32 = jnp.float32


def tables(blocks):
    period = 2 * blocks * LANES
    chips = blocks // 4
    order = np.array([4 * j + tb for tb in range(4) for j in range(chips)])
    freq = np.arange(blocks) + 0.5
    lane = np.arange(LANES)
    angle = 2.0 * math.pi * freq[:, None] * order[None, :] / (2 * blocks)
    first = np.concatenate([np.cos(angle), -np.sin(angle)], axis=0)
    turn = 2.0 * math.pi * freq[:, None] * lane[None, :] / period
    inner = 2.0 * math.pi * ((lane[:, None] * lane[None, :]) % LANES) / LANES
    cosine, sine = np.cos(inner), np.sin(inner)
    middle = np.block([[cosine, -sine], [sine, cosine]])
    last = first.T * (2.0 / period)

    def parts(table, axis):
        high = table.astype(ml_dtypes.bfloat16)
        low = (table - high.astype(np.float64)).astype(ml_dtypes.bfloat16)
        return np.concatenate([high, low, high], axis=axis)

    return (
        parts(first, 1),
        parts(middle, 0),
        parts(middle.T, 0),
        parts(last, 1),
        np.cos(turn).astype(np.float32),
        np.sin(turn).astype(np.float32),
    )


def matmul(left, right, dims=((1,), (0,))):
    return lax.dot_general(left, right, (dims, ((), ())), preferred_element_type=F32)


def split(value):
    high = value.astype(BF16)
    low = (value - high.astype(F32)).astype(BF16)
    return high, low


def greet(me, peers, group, groups):
    barrier = pltpu.get_barrier_semaphore()

    def one(step, carry):
        pl.semaphore_signal(
            barrier, inc=1, device_id=(lax.rem(me + step, peers), group), device_id_type=MESH
        )
        return carry

    lax.fori_loop(1, peers, one, 0)
    for step in range(1, groups):
        pl.semaphore_signal(
            barrier, inc=1, device_id=(me, lax.rem(group + step, groups)), device_id_type=MESH
        )
    return barrier


def wait_bytes(ref, sem):
    pltpu.make_async_copy(ref, ref, sem).wait()


def send(src, dst, sem_out, sem_in, seq, chan):
    pltpu.make_async_remote_copy(
        src_ref=src, dst_ref=dst, send_sem=sem_out, recv_sem=sem_in,
        device_id=(seq, chan), device_id_type=MESH,
    ).start()


def layer_kernel(
    n, groups, x_ref, w_ref, filters_ref, cot_ref, bias_ref,
    first_ref, middle_ref, middle_t_ref, last_ref, cos_ref, sin_ref,
    b_back, w_own, w_far, u_own, u_recv,
    wg, w_other, xg, xt, total, stage_a, a_send, a_recv, stage_b, b_send, b_recv,
    spec_h1, spec_h2, spec_v, spec_z, spec_g1, spec_g2,
    stage_c, g_send, g_recv, stage_d, b_give, turned_ref, grad, grad_in,
    w_send, w_in, w_relay, u_acc, u_send,
    sems, x_sems, xp_sems, u_sems, gs_sems, g_sems, c_sems, ws_sems, w_sems, bs_sems, b_sems,
):
    me = lax.axis_index("seq")
    group = lax.axis_index("chan")
    core = lax.rem(me, 2)
    chip = me // 2
    partner = me + 1 - 2 * core
    chips = n // 2
    ny = min(4, chips // 2)
    nx = chips // (2 * ny)
    plane = nx * ny
    y = lax.rem(chip, ny)
    zl = lax.rem(chip // ny, 2)
    xx = chip // (2 * ny)
    here = (xx * ny + y) * 2 + core
    quota = LANES // chips
    blocks = 4 * chips
    rows_a, rows_b = a_send.shape[1], b_send.shape[1]
    rows_c = 4 * quota
    tokens, depth = x_ref.shape
    cols = wg.shape[2]
    slots = depth // wg.shape[1]

    def in_plane(p, c, z):
        return (((p // ny) * 2 + z) * ny + lax.rem(p, ny)) * 2 + c

    barrier = greet(me, n, group, groups)

    def spread(value, base):
        turned = value.T
        for half in range(2):
            for q in range(quota):
                top = half * LANES + q * chips
                for tb in range(2):
                    stage_b[pl.ds(half * rows_b + base + q * 2 + tb, chips, stride=2 * rows_b), :] = turned[
                        top : top + chips, tb * LANES : (tb + 1) * LANES
                    ]

    spread(filters_ref[0], 0)
    spread(filters_ref[1], 2 * quota)
    spread(cot_ref[...].astype(F32), 4 * quota)
    for peer in range(n):
        stage_b[pl.ds(peer * rows_b + 6 * quota, 2 * quota), :] = jnp.zeros((2 * quota, LANES), F32)
    b_send[...] = stage_b[...].astype(BF16).reshape(b_send.shape)
    xg[core, group] = x_ref[...]
    pl.semaphore_wait(barrier, n - 1 + groups - 1)

    near = [step for step in range(1, groups) if min(step, groups - step) == 1]
    far = [step for step in range(1, groups) if min(step, groups - step) > 1]
    for step in far + near:
        send(x_ref, xg.at[core, group], sems.at[2], x_sems.at[group], me, lax.rem(group + step, groups))
    z_first = in_plane(xx * ny + y, 0, 1 - zl)
    for c in range(2):
        send(w_ref.at[c], wg.at[me], sems.at[0], sems.at[3], z_first + c, group)

    def send_w(step, carry):
        peer = lax.rem(here + step, 2 * plane)
        c = lax.rem(peer, 2)
        send(w_ref.at[c], wg.at[me], sems.at[0], sems.at[1], in_plane(peer // 2, c, zl), group)
        return carry

    lax.fori_loop(1, 2 * plane, send_w, 0)
    pltpu.make_async_copy(w_ref.at[core], wg.at[me], sems.at[1]).start()
    send(x_ref, xg.at[core, group], sems.at[2], xp_sems.at[group], partner, group)
    wait_bytes(wg.at[pl.ds(z_first, 2)], sems.at[3])

    def forward_w(step, carry):
        p = lax.rem(here // 2 + step, plane)
        part = wg.at[pl.ds(z_first, 2)]
        send(part, part, sems.at[4], sems.at[5], in_plane(p, core, zl), group)
        return carry

    lax.fori_loop(1, plane, forward_w, 0)

    def relay(step):
        other = lax.rem(group + groups - step, groups)
        wait_bytes(xg.at[core, other], x_sems.at[other])
        part = xg.at[core, other]
        send(part, part, sems.at[6], xp_sems.at[other], partner, group)

    for step in near:
        relay(step)
    wait_bytes(wg.at[pl.ds(0, 2 * plane)], sems.at[1])
    wait_bytes(wg.at[pl.ds(0, 2 * plane - 2)], sems.at[5])
    send(wg, w_other, sems.at[7], sems.at[8], partner, group)

    def give_b(step, carry):
        peer = lax.rem(me + step, n)
        send(b_send.at[peer], b_recv.at[me], sems.at[9], sems.at[10], peer, group)
        return carry

    lax.fori_loop(1, n, give_b, 0)
    pltpu.make_async_copy(b_send.at[me], b_recv.at[me], sems.at[10]).start()

    def weights(ref, c):
        return ref[pl.ds(c * slots, slots)].reshape(depth, cols)

    def project(side, step):
        other = lax.rem(group + groups - step, groups)
        if side == 1:
            wait_bytes(xg.at[1 - core, other], xp_sems.at[other])
        at = core if side == 0 else 1 - core
        term = matmul(xg[at, other], weights(wg, other))
        total[at] = term if step == 0 else total[at] + term

    for step in [0] + near:
        project(0, step)
    for step in [0] + near:
        project(1, step)
    for step in far:
        relay(step)
        project(0, step)
    for step in far:
        project(1, step)
    turned = total[...].reshape(2 * tokens, cols).T
    for a in range(3):
        for q in range(quota):
            top = a * LANES + q * chips
            for tb in range(4):
                stage_a[pl.ds((a * quota + q) * 4 + tb, chips, stride=rows_a), :] = turned[
                    top : top + chips, tb * LANES : (tb + 1) * LANES
                ]
    a_send[...] = stage_a[...].astype(BF16).reshape(a_send.shape)

    def give_a(step, carry):
        peer = lax.rem(chip + step, chips)
        send(a_send.at[peer], a_recv.at[chip], sems.at[11], sems.at[12], 2 * peer + core, group)
        return carry

    lax.fori_loop(1, chips, give_a, 0)
    pltpu.make_async_copy(a_send.at[chip], a_recv.at[chip], sems.at[12]).start()

    def columns(ref, start, stride):
        return jnp.concatenate(
            [
                jnp.concatenate(
                    [ref[pl.ds(start(q, tb), chips, stride=stride), :] for q in range(quota)], axis=1
                )
                for tb in range(4)
            ],
            axis=0,
        )

    def late(a):
        return columns(stage_a, lambda q, tb: (a * quota + q) * 4 + tb, rows_a)

    def early(base):
        return columns(stage_b, lambda q, tb: (tb // 2) * rows_b + base + q * 2 + tb % 2, 2 * rows_b)

    def piece(value, q):
        return value[:, q * LANES : (q + 1) * LANES]

    def forward(value, spec, exact=False):
        high, low = split(value)
        if exact:
            wide = matmul(first_ref[:, : 2 * blocks], jnp.concatenate([high, high], axis=0))
        else:
            wide = matmul(first_ref[...], jnp.concatenate([high, high, low], axis=0))
        turn_cos, turn_sin = cos_ref[...], sin_ref[...]
        for q in range(quota):
            re = piece(wide[:blocks], q)
            im = piece(wide[blocks:], q)
            high, low = split(
                jnp.concatenate([re * turn_cos + im * turn_sin, im * turn_cos - re * turn_sin], axis=1)
            )
            spec[q * blocks : (q + 1) * blocks, :] = matmul(
                jnp.concatenate([high, high, low], axis=1), middle_ref[...]
            )

    def backward(left, right, conj_left, conj_right):
        turn_cos, turn_sin = cos_ref[...], sin_ref[...]
        columns_high, columns_low = [], []
        for q in range(quota):
            rows = slice(q * blocks, (q + 1) * blocks)
            l_re, l_im = left[rows, :LANES], left[rows, LANES:]
            r_re, r_im = right[rows, :LANES], right[rows, LANES:]
            cross = l_im * r_im
            y_re = l_re * r_re - (cross if conj_left == conj_right else -cross)
            if conj_left:
                y_im = l_re * r_im - l_im * r_re
            elif conj_right:
                y_im = l_im * r_re - l_re * r_im
            else:
                y_im = l_re * r_im + l_im * r_re
            high, low = split(jnp.concatenate([y_re, y_im], axis=1))
            out = matmul(jnp.concatenate([high, high, low], axis=1), middle_t_ref[...])
            re, im = out[:, :LANES], out[:, LANES:]
            high, low = split(
                jnp.concatenate([re * turn_cos - im * turn_sin, im * turn_cos + re * turn_sin], axis=0)
            )
            columns_high.append(high)
            columns_low.append(low)
        high = jnp.concatenate(columns_high, axis=1)
        low = jnp.concatenate(columns_low, axis=1)
        return matmul(last_ref[...], jnp.concatenate([high, high, low], axis=0))

    def skip(f):
        return jnp.concatenate(
            [
                jnp.full((1, LANES), bias_ref[f, core * LANES + q * chips + chip], F32)
                for q in range(quota)
            ],
            axis=1,
        )

    def give_late(value, a):
        for q in range(quota):
            for tb in range(4):
                stage_c[pl.ds(q * 4 + tb, chips, stride=rows_c), :] = piece(value, q)[
                    tb * chips : (tb + 1) * chips
                ]
        g_send[a] = stage_c[...].astype(BF16).reshape(chips, rows_c, LANES)

        def one(step, carry):
            peer = lax.rem(chip + step, chips)
            send(g_send.at[a, peer], g_recv.at[a, chip], gs_sems.at[a], g_sems.at[a], 2 * peer + core, group)
            return carry

        lax.fori_loop(1, chips, one, 0)
        pltpu.make_async_copy(g_send.at[a, chip], g_recv.at[a, chip], g_sems.at[a]).start()

    def put_early(value, base):
        for q in range(quota):
            for tb in range(4):
                at = (tb // 2) * rows_c + base + q * 2 + tb % 2
                stage_d[pl.ds(at, chips, stride=2 * rows_c), :] = piece(value, q)[
                    tb * chips : (tb + 1) * chips
                ]

    def put_skip(product, f):
        lane = lax.broadcasted_iota(jnp.int32, (1, LANES), 1)
        sums = jnp.sum(product, axis=0, keepdims=True)
        for q in range(quota):
            value = jnp.sum(piece(sums, q), axis=1, keepdims=True)
            one = value.astype(BF16).astype(F32)
            two = (value - one).astype(BF16).astype(F32)
            three = value - one - two
            row = jnp.where(lane == chip, one, 0.0)
            row = jnp.where(lane == chips + chip, two, row)
            row = jnp.where(lane == 2 * chips + chip, three, row)
            for half in range(2):
                at = half * rows_c + 2 * quota + f * quota + q
                stage_d[pl.ds(at, chips, stride=2 * rows_c), :] = jnp.broadcast_to(row, (chips, LANES))

    def give_early(k):
        b_give[k] = stage_d[...].astype(BF16).reshape(n, rows_c, LANES)

        def one(step, carry):
            peer = lax.rem(me + step, n)
            send(b_give.at[k, peer], b_back.at[k, me], bs_sems.at[k], b_sems.at[k], peer, group)
            return carry

        lax.fori_loop(1, n, one, 0)
        pltpu.make_async_copy(b_give.at[k, me], b_back.at[k, me], b_sems.at[k]).start()

    wait_bytes(b_recv, sems.at[10])
    stage_b[...] = b_recv[...].reshape(stage_b.shape).astype(F32)
    forward(early(0), spec_h1, True)
    forward(early(2 * quota), spec_h2, True)
    for c in range(groups):
        xt[c] = xg[:, c].reshape(2 * tokens, depth).astype(F32).T.astype(BF16)
    wait_bytes(a_recv, sems.at[12])
    stage_a[...] = a_recv[...].reshape(stage_a.shape).astype(F32)
    values_v, gate_one, gate_two = late(0), late(1), late(2)
    grad_out = early(4 * quota)
    skip_one, skip_two = skip(0), skip(1)
    forward(values_v, spec_v, True)
    conv_one = backward(spec_h1, spec_v, False, False) + skip_one * values_v
    mixed = gate_one * conv_one
    grad_conv_two = grad_out * gate_two
    forward(grad_conv_two, spec_g2)
    grad_mixed = backward(spec_h2, spec_g2, True, False) + skip_two * grad_conv_two
    give_late(grad_mixed * conv_one, 1)
    grad_conv_one = grad_mixed * gate_one
    forward(grad_conv_one, spec_g1)
    give_late(backward(spec_h1, spec_g1, True, False) + skip_one * grad_conv_one, 0)
    forward(mixed, spec_z)
    conv_two = backward(spec_h2, spec_z, False, False) + skip_two * mixed
    give_late(grad_out * conv_two, 2)
    put_early(gate_two * conv_two, 0)
    put_early(backward(spec_g2, spec_z, False, True), 2 * quota)
    give_early(0)
    put_early(backward(spec_g1, spec_v, False, True), 0)
    put_skip(grad_conv_one * values_v, 0)
    put_skip(grad_conv_two * mixed, 1)
    give_early(1)

    def take(a):
        wait_bytes(g_recv.at[a], g_sems.at[a])
        stage_c[...] = g_recv[a].reshape(stage_c.shape).astype(F32)
        for q in range(quota):
            for tb in range(4):
                turned_ref[q * chips : (q + 1) * chips, tb * LANES : (tb + 1) * LANES] = stage_c[
                    pl.ds(q * 4 + tb, chips, stride=rows_c), :
                ]
        grad[a] = turned_ref[...].T.astype(BF16).reshape(2, tokens, LANES)
        send(grad.at[a, 1 - core], grad_in.at[a], sems.at[13], c_sems.at[a], partner, group)

    def give_w(a):
        block = grad[a].reshape(2 * tokens, LANES)
        per = n // groups
        for c in range(groups):
            term = matmul(xt[c], block).astype(BF16).reshape(slots, depth // slots, LANES)
            for k in range(slots):
                s = c * slots + k
                w_send[a, s // (4 * ny), (s // (2 * ny)) % 2, s % (2 * ny)] = term[k]

        def one(step, carry):
            peer = lax.rem(here + step, 2 * plane)
            p, c = peer // 2, lax.rem(peer, 2)
            send(
                w_send.at[a, p // ny, :, lax.rem(p, ny) * 2 + c], w_in.at[a, here],
                ws_sems.at[a], w_sems.at[a], in_plane(p, c, zl), group,
            )
            return carry

        lax.fori_loop(1, 2 * plane, one, 0)
        pltpu.make_async_copy(w_send.at[a, xx, :, y * 2 + core], w_in.at[a, here], w_sems.at[a]).start()

    def both(arrays, c):
        left = jnp.concatenate([part for a in arrays for part in (grad[a, core], grad_in[a])], axis=1)
        wide = [weights(wg, c), weights(w_other, c)]
        right = jnp.concatenate([piece(part, a) for a in arrays for part in wide], axis=1)
        return matmul(left, right, ((1,), (1,)))

    take(1)
    give_w(1)
    take(0)
    give_w(0)
    wait_bytes(w_other, sems.at[8])
    for a in (1, 0):
        wait_bytes(grad_in.at[a], c_sems.at[a])
    for c in range(groups):
        u_acc[c] = both((1, 0), c)
    take(2)
    wait_bytes(grad_in.at[2], c_sems.at[2])
    for c in range(groups):
        value = u_acc[c] + both((2,), c)
        u_acc[c] = value
        u_send[c] = value.astype(BF16)
    for step in far + near:
        other = lax.rem(group + step, groups)
        send(u_send.at[other], u_recv.at[group], sems.at[14], u_sems.at[group], me, other)
    give_w(2)
    u_own[...] = u_acc[group]

    z_device = z_first + core
    for a in (1, 0, 2):
        wait_bytes(w_in.at[a], w_sems.at[a])
        for half in range(2):
            own = w_in[a, half, zl].astype(F32)
            away = w_in[a, half, 1 - zl].astype(F32)
            for p in range(1, plane):
                own = own + w_in[a, 2 * p + half, zl].astype(F32)
                away = away + w_in[a, 2 * p + half, 1 - zl].astype(F32)
            w_own[a, half] = own
            w_relay[a, half] = away
        send(w_relay.at[a], w_far.at[a], sems.at[15], sems.at[16], z_device, group)

    wait_bytes(b_back.at[0], b_sems.at[0])
    wait_bytes(b_back.at[1], b_sems.at[1])
    for step in near + far:
        other = lax.rem(group + groups - step, groups)
        wait_bytes(u_recv.at[other], u_sems.at[other])
    wait_bytes(w_far, sems.at[16])
    wait_bytes(wg.at[pl.ds(0, 2 * plane + 1)], sems.at[0])
    wait_bytes(xg.at[0], sems.at[2])
    wait_bytes(wg.at[pl.ds(0, 2 * plane - 2)], sems.at[4])
    if groups > 1:
        wait_bytes(xg.at[0, pl.ds(0, groups - 1)], sems.at[6])
        wait_bytes(u_recv.at[pl.ds(0, groups - 1)], sems.at[14])
    wait_bytes(wg, sems.at[7])
    wait_bytes(b_recv.at[pl.ds(0, n - 1)], sems.at[9])
    wait_bytes(a_recv.at[pl.ds(0, chips - 1)], sems.at[11])
    wait_bytes(grad_in, sems.at[13])
    wait_bytes(w_far, sems.at[15])
    for a in range(3):
        wait_bytes(g_recv.at[a, pl.ds(0, chips - 1)], gs_sems.at[a])
        wait_bytes(w_in.at[a, pl.ds(0, 2 * plane - 1)], ws_sems.at[a])
    for k in range(2):
        wait_bytes(b_back.at[k, pl.ds(0, n - 1)], bs_sems.at[k])


def finish_kernel(
    n, groups, b_back, w_own, w_far, u_own, u_recv, out_ref, gu_ref, gw_ref, gf_ref, gb_ref, stage, turned_ref
):
    group = lax.axis_index("chan")
    chips = n // 2
    quota = LANES // chips
    rows_c = 4 * quota

    def collect(k, base):
        for half in range(2):
            for q in range(quota):
                top = half * LANES + q * chips
                for tb in range(2):
                    turned_ref[top : top + chips, tb * LANES : (tb + 1) * LANES] = stage[
                        k, pl.ds(half * rows_c + base + q * 2 + tb, chips, stride=2 * rows_c), :
                    ]
        return turned_ref[...].T

    stage[...] = b_back[...].reshape(stage.shape).astype(F32)
    out_ref[...] = collect(0, 0).astype(BF16)
    gf_ref[1] = collect(0, 2 * quota)
    gf_ref[0] = collect(1, 0)
    lane = lax.broadcasted_iota(jnp.int32, (1, LANES), 1)
    for f in range(2):
        for half in range(2):
            line = jnp.zeros((1, LANES), F32)
            for q in range(quota):
                at = half * rows_c + 2 * quota + f * quota + q
                row = jnp.sum(stage[1, pl.ds(at, chips, stride=2 * rows_c), :], axis=0, keepdims=True)
                full = row + pltpu.roll(row, LANES - chips, 1) + pltpu.roll(row, LANES - 2 * chips, 1)
                moved = full if q == 0 else pltpu.roll(full, q * chips, 1)
                line = jnp.where((lane >= q * chips) & (lane < (q + 1) * chips), moved, line)
            gb_ref[f : f + 1, half * LANES : (half + 1) * LANES] = line
    total = u_own[...]
    for step in range(1, groups):
        total = total + u_recv[lax.rem(group + step, groups)].astype(F32)
    gu_ref[...] = total.astype(BF16)
    for a in range(3):
        for half in range(2):
            gw_ref[:, a, half * LANES : (half + 1) * LANES] = w_own[a, half] + w_far[a, half]


def on_device(layer_input, w_in, filters, bias, cotangent):
    n = lax.axis_size("seq")
    groups = lax.axis_size("chan")
    tokens, width = layer_input.shape
    rows = w_in.shape[0]
    chips = n // 2
    ny = min(4, chips // 2)
    nx = chips // (2 * ny)
    plane = nx * ny
    quota = LANES // chips
    blocks = 4 * chips
    rows_a, rows_b, rows_c = 12 * quota, 8 * quota, 4 * quota
    cols = 3 * LANES
    vmem = pl.BlockSpec(memory_space=pltpu.VMEM)
    smem = pl.BlockSpec(memory_space=pltpu.SMEM)
    sds = jax.ShapeDtypeStruct
    dma = pltpu.SemaphoreType.DMA
    limit = 58 * 1024 * 1024
    spec = pltpu.VMEM((quota * blocks, 2 * LANES), F32)

    w_halves = w_in.reshape(rows, 3, 2, LANES).transpose(2, 0, 1, 3).reshape(2, rows, cols)
    landed = pl.pallas_call(
        functools.partial(layer_kernel, n, groups),
        out_shape=(
            sds((2, n, rows_c, LANES), BF16),
            sds((3, 2, rows, LANES), F32),
            sds((3, 2, rows, LANES), F32),
            sds((tokens, width), F32),
            sds((groups, tokens, width), BF16),
        ),
        in_specs=[vmem] * 4 + [smem] + [vmem] * 6,
        out_specs=(vmem,) * 5,
        scratch_shapes=[
            pltpu.VMEM((n, rows, cols), BF16),
            pltpu.VMEM((n, rows, cols), BF16),
            pltpu.VMEM((2, groups, tokens, width), BF16),
            pltpu.VMEM((groups, width, 2 * tokens), BF16),
            pltpu.VMEM((2, tokens, cols), F32),
            pltpu.VMEM((chips * rows_a, LANES), F32),
            pltpu.VMEM((chips, rows_a, LANES), BF16),
            pltpu.VMEM((chips, rows_a, LANES), BF16),
            pltpu.VMEM((n * rows_b, LANES), F32),
            pltpu.VMEM((n, rows_b, LANES), BF16),
            pltpu.VMEM((n, rows_b, LANES), BF16),
            spec, spec, spec, spec, spec, spec,
            pltpu.VMEM((chips * rows_c, LANES), F32),
            pltpu.VMEM((3, chips, rows_c, LANES), BF16),
            pltpu.VMEM((3, chips, rows_c, LANES), BF16),
            pltpu.VMEM((n * rows_c, LANES), F32),
            pltpu.VMEM((2, n, rows_c, LANES), BF16),
            pltpu.VMEM((LANES, 2 * tokens), F32),
            pltpu.VMEM((3, 2, tokens, LANES), BF16),
            pltpu.VMEM((3, tokens, LANES), BF16),
            pltpu.VMEM((3, nx, 2, 2 * ny, rows, LANES), BF16),
            pltpu.VMEM((3, 2 * plane, 2, rows, LANES), BF16),
            pltpu.VMEM((3, 2, rows, LANES), F32),
            pltpu.VMEM((groups, tokens, width), F32),
            pltpu.VMEM((groups, tokens, width), BF16),
            dma((17,)),
            dma((groups,)), dma((groups,)), dma((groups,)),
            dma((3,)), dma((3,)), dma((3,)), dma((3,)), dma((3,)),
            dma((2,)), dma((2,)),
        ],
        compiler_params=pltpu.CompilerParams(
            collective_id=0, has_side_effects=True, vmem_limit_bytes=limit
        ),
        name="layer",
    )(layer_input, w_halves, filters, cotangent, bias, *(jnp.asarray(table) for table in tables(blocks)))

    return pl.pallas_call(
        functools.partial(finish_kernel, n, groups),
        out_shape=(
            sds((tokens, width), BF16),
            sds((tokens, width), BF16),
            sds((rows, 3, width), F32),
            sds((2, tokens, width), F32),
            sds((2, width), F32),
        ),
        in_specs=[vmem] * 5,
        out_specs=(vmem,) * 5,
        scratch_shapes=[
            pltpu.VMEM((2, n * rows_c, LANES), F32),
            pltpu.VMEM((2 * LANES, tokens), F32),
        ],
        compiler_params=pltpu.CompilerParams(vmem_limit_bytes=limit // 4),
        name="finish",
    )(*landed)


def solution(mesh):
    in_specs = (
        P("seq", "chan"),
        P("seq", None, "chan"),
        P(None, "seq", "chan"),
        P(None, "chan"),
        P("seq", "chan"),
    )
    out_specs = (
        P("seq", "chan"),
        P("seq", "chan"),
        P("seq", None, "chan"),
        P(None, "seq", "chan"),
        P(None, "chan"),
    )
    return jax.shard_map(
        on_device, mesh=mesh, in_specs=in_specs, out_specs=out_specs, check_vma=False
    )
```

time: 103 us -> 86.8 us (0.84)
  Pallas kernels: 94.4 us -> 79.1 us
    pallas_call x3 -> x2, Pallas kernels: 94.4 us -> 79.1 us  [the longest x1 77.4 us: on_device(): pl.pallas_call(functools.partial(layer_kernel, n, groups), out_shape=(sds...]
    reshape x2 -> x0, local copies, waits for them, and re-layouts: 1.54 us -> none  [on_device(): grad_w.reshape(2, rows, 3, LANES).transpose(1, 2, 0, 3)]
    unnamed x8 -> x10, local copies, waits for them, and re-layouts: 4.51 us -> 4.62 us
where the time goes in v2:
time: 86.8 us; the launch traced here: 86.4 us
  Pallas kernels  79.1 us (91%)
  local copies, waits for them, and re-layouts  6.66 us (8%)
    pallas_call x1, Pallas kernels, on_device(): pl.pallas_call(functools.partial(layer_kernel, n, groups), out_shape=(sds...  77.4 us
    unnamed x10, local copies, waits for them, and re-layouts  4.62 us

profile of v2, /device:TPU:1, one launch (start us, length us, event | category | flops | bytes accessed | tf_op | source)
XLA Modules:
  0.0 86.4 jit_solution(11001287928822671457)
XLA Ops:
  0.6 0.8 reshape.16
  1.4 0.6 reshape.17.w_ref
  2.0 77.4 %layer.1 = (bf16[2,64,16,128]{3,2,1,0:T(8,128)(2,1)}, f32[3,2,16,128]{3,2,1,0:T(8,128)}, f32[3,2,16,128]{3,2,1,0:T(8,128)}, f32[256,256]{1,0:T(8,128)}, bf16[4,256,256]{2,1,0:T(8,128)(2,1)}) custom-call(bf16[256,256]{1,0:T(8,128)(2,1)} %x_ref.1, bf16[2,16,384]{2,1,0:T(8,128)(2,1)} %reshape.17.w_ref, f32[2,256,256]{2,1,0:T(8,128)} %filters_ref.1, ...), custom_call_target="tpu_custom_call" | custom-call | tf_op jit(solution)/shard_map/layer/pallas_call | solution.py:540
  79.5 0.0 copy-start
  79.5 1.0 %copy-done = bf16[2,64,16,128]{3,2,1,0:T(8,128)(2,1)S(1)} copy-done((bf16[2,64,16,128]{3,2,1,0:T(8,128)(2,1)S(1)}, bf16[2,64,16,128]{3,2,1,0:T(8,128)(2,1)}, u32[]{:S(2)}) %copy-start) | copy-done | bytes 524312
  80.5 0.0 copy-start.1
  80.5 1.0 %copy-done.1 = bf16[4,256,256]{2,1,0:T(8,128)(2,1)S(1)} copy-done((bf16[4,256,256]{2,1,0:T(8,128)(2,1)S(1)}, bf16[4,256,256]{2,1,0:T(8,128)(2,1)}, u32[]{:S(2)}) %copy-start.1) | copy-done | bytes 524312
  81.6 0.0 copy-start.2
  81.6 0.9 %copy-done.2 = f32[256,256]{1,0:T(8,128)S(1)} copy-done((f32[256,256]{1,0:T(8,128)S(1)}, f32[256,256]{1,0:T(8,128)}, u32[]{:S(2)}) %copy-start.2) | copy-done | bytes 262168
  82.5 0.0 copy-start.3
  82.5 0.8 copy-done.3
  83.3 0.0 copy-start.4
  83.3 0.8 copy-done.4
  84.1 1.6 %finish.1 = (bf16[256,256]{1,0:T(8,128)(2,1)}, bf16[256,256]{1,0:T(8,128)(2,1)}, f32[16,3,256]{2,1,0:T(4,128)S(1)}, f32[2,256,256]{2,1,0:T(8,128)}, f32[2,256]{1,0:T(2,128)}) custom-call(bf16[2,64,16,128]{3,2,1,0:T(8,128)(2,1)S(1)} %copy-done, f32[3,2,16,128]{3,2,1,0:T(8,128)S(1)} %copy-done.3, f32[3,2,16,128]{3,2,1,0:T(8,128)S(1)} %copy-done.4, ...), custom_call_target="tpu_custom_call" | custom-call | tf_op jit(solution)/shard_map/finish/pallas_call | solution.py:588
  85.8 0.6 copy.19
  (1 shorter events, 0.0 us)
Async XLA Ops:
  79.5 1.0 %copy-start = (bf16[2,64,16,128]{3,2,1,0:T(8,128)(2,1)S(1)}, bf16[2,64,16,128]{3,2,1,0:T(8,128)(2,1)}, u32[]{:S(2)}) copy-start(bf16[2,64,16,128]{3,2,1,0:T(8,128)(2,1)} %get-tuple-element.10.b_back) | copy-start | bytes 1572868
  80.5 1.0 %copy-start.1 = (bf16[4,256,256]{2,1,0:T(8,128)(2,1)S(1)}, bf16[4,256,256]{2,1,0:T(8,128)(2,1)}, u32[]{:S(2)}) copy-start(bf16[4,256,256]{2,1,0:T(8,128)(2,1)} %get-tuple-element.14.u_recv) | copy-start | bytes 1572868
  81.6 0.9 %copy-start.2 = (f32[256,256]{1,0:T(8,128)S(1)}, f32[256,256]{1,0:T(8,128)}, u32[]{:S(2)}) copy-start(f32[256,256]{1,0:T(8,128)} %get-tuple-element.13.u_own) | copy-start | bytes 786436
  82.5 0.8 copy-start.3
  83.3 0.8 copy-start.4

commit v3 on v2

--- a/solution.py
+++ b/solution.py
@@ -84,14 +84,14 @@
 
 
 def layer_kernel(
-    n, groups, x_ref, w_ref, filters_ref, cot_ref, bias_ref,
+    n, groups, x_ref, w_in_ref, filters_ref, cot_ref, bias_ref,
     first_ref, middle_ref, middle_t_ref, last_ref, cos_ref, sin_ref,
     b_back, w_own, w_far, u_own, u_recv,
-    wg, w_other, xg, xt, total, stage_a, a_send, a_recv, stage_b, b_send, b_recv,
+    w_ref, wg, w_other, xg, xt, total, stage_a, a_send, a_recv, stage_b, b_send, b_recv,
     spec_h1, spec_h2, spec_v, spec_z, spec_g1, spec_g2,
     stage_c, g_send, g_recv, stage_d, b_give, turned_ref, grad, grad_in,
     w_send, w_in, w_relay, u_acc, u_send,
-    sems, x_sems, xp_sems, u_sems, gs_sems, g_sems, c_sems, ws_sems, w_sems, bs_sems, b_sems,
+    sems, x_sems, xp_sems, xr_sems, u_sems, gs_sems, g_sems, cs_sems, c_sems, bs_sems, b_sems, ws_sems, w_sems,
 ):
     me = lax.axis_index("seq")
     group = lax.axis_index("chan")
@@ -117,7 +117,19 @@
     def in_plane(p, c, z):
         return (((p // ny) * 2 + z) * ny + lax.rem(p, ny)) * 2 + c
 
+    pending = {}
+
+    def expect(key, ref, sem):
+        pending[key] = (ref, sem)
+
+    def arrive(*key):
+        wait_bytes(*pending.pop(key))
+
     barrier = greet(me, n, group, groups)
+
+    for half in range(2):
+        for a in range(3):
+            w_ref[half, :, a * LANES : (a + 1) * LANES] = w_in_ref[a, :, half * LANES : (half + 1) * LANES]
 
     def spread(value, base):
         turned = value.T
@@ -142,6 +154,9 @@
     far = [step for step in range(1, groups) if min(step, groups - step) > 1]
     for step in far + near:
         send(x_ref, xg.at[core, group], sems.at[2], x_sems.at[group], me, lax.rem(group + step, groups))
+    for step in range(1, groups):
+        other = lax.rem(group + groups - step, groups)
+        expect(("x", step), xg.at[core, other], x_sems.at[other])
     z_first = in_plane(xx * ny + y, 0, 1 - zl)
     for c in range(2):
         send(w_ref.at[c], wg.at[me], sems.at[0], sems.at[3], z_first + c, group)
@@ -155,6 +170,10 @@
     lax.fori_loop(1, 2 * plane, send_w, 0)
     pltpu.make_async_copy(w_ref.at[core], wg.at[me], sems.at[1]).start()
     send(x_ref, xg.at[core, group], sems.at[2], xp_sems.at[group], partner, group)
+    expect(("x out",), xg.at[0], sems.at[2])
+    expect(("w",), wg.at[pl.ds(0, 2 * plane)], sems.at[1])
+    expect(("w out",), wg.at[pl.ds(0, 2 * plane + 1)], sems.at[0])
+    expect(("xp", 0), xg.at[1 - core, group], xp_sems.at[group])
     wait_bytes(wg.at[pl.ds(z_first, 2)], sems.at[3])
 
     def forward_w(step, carry):
@@ -164,18 +183,24 @@
         return carry
 
     lax.fori_loop(1, plane, forward_w, 0)
+    expect(("w rest",), wg.at[pl.ds(0, 2 * plane - 2)], sems.at[5])
+    expect(("w rest out",), wg.at[pl.ds(0, 2 * plane - 2)], sems.at[4])
 
     def relay(step):
         other = lax.rem(group + groups - step, groups)
-        wait_bytes(xg.at[core, other], x_sems.at[other])
+        arrive("x", step)
         part = xg.at[core, other]
-        send(part, part, sems.at[6], xp_sems.at[other], partner, group)
+        send(part, part, xr_sems.at[step], xp_sems.at[other], partner, group)
+        expect(("xp", step), xg.at[1 - core, other], xp_sems.at[other])
+        expect(("x relay", step), xg.at[1 - core, other], xr_sems.at[step])
 
     for step in near:
         relay(step)
-    wait_bytes(wg.at[pl.ds(0, 2 * plane)], sems.at[1])
-    wait_bytes(wg.at[pl.ds(0, 2 * plane - 2)], sems.at[5])
+    arrive("w")
+    arrive("w rest")
     send(wg, w_other, sems.at[7], sems.at[8], partner, group)
+    expect(("other",), w_other, sems.at[8])
+    expect(("other out",), w_other, sems.at[7])
 
     def give_b(step, carry):
         peer = lax.rem(me + step, n)
@@ -184,6 +209,8 @@
 
     lax.fori_loop(1, n, give_b, 0)
     pltpu.make_async_copy(b_send.at[me], b_recv.at[me], sems.at[10]).start()
+    expect(("b",), b_recv, sems.at[10])
+    expect(("b out",), b_recv.at[pl.ds(0, n - 1)], sems.at[9])
 
     def weights(ref, c):
         return ref[pl.ds(c * slots, slots)].reshape(depth, cols)
@@ -191,7 +218,7 @@
     def project(side, step):
         other = lax.rem(group + groups - step, groups)
         if side == 1:
-            wait_bytes(xg.at[1 - core, other], xp_sems.at[other])
+            arrive("xp", step)
         at = core if side == 0 else 1 - core
         term = matmul(xg[at, other], weights(wg, other))
         total[at] = term if step == 0 else total[at] + term
@@ -222,6 +249,8 @@
 
     lax.fori_loop(1, chips, give_a, 0)
     pltpu.make_async_copy(a_send.at[chip], a_recv.at[chip], sems.at[12]).start()
+    expect(("a",), a_recv, sems.at[12])
+    expect(("a out",), a_recv.at[pl.ds(0, chips - 1)], sems.at[11])
 
     def columns(ref, start, stride):
         return jnp.concatenate(
@@ -311,6 +340,8 @@
 
         lax.fori_loop(1, chips, one, 0)
         pltpu.make_async_copy(g_send.at[a, chip], g_recv.at[a, chip], g_sems.at[a]).start()
+        expect(("g", a), g_recv.at[a], g_sems.at[a])
+        expect(("g out", a), g_recv.at[a, pl.ds(0, chips - 1)], gs_sems.at[a])
 
     def put_early(value, base):
         for q in range(quota):
@@ -345,14 +376,16 @@
 
         lax.fori_loop(1, n, one, 0)
         pltpu.make_async_copy(b_give.at[k, me], b_back.at[k, me], b_sems.at[k]).start()
-
-    wait_bytes(b_recv, sems.at[10])
+        expect(("back", k), b_back.at[k], b_sems.at[k])
+        expect(("back out", k), b_back.at[k, pl.ds(0, n - 1)], bs_sems.at[k])
+
+    arrive("b")
     stage_b[...] = b_recv[...].reshape(stage_b.shape).astype(F32)
     forward(early(0), spec_h1, True)
     forward(early(2 * quota), spec_h2, True)
     for c in range(groups):
         xt[c] = xg[:, c].reshape(2 * tokens, depth).astype(F32).T.astype(BF16)
-    wait_bytes(a_recv, sems.at[12])
+    arrive("a")
     stage_a[...] = a_recv[...].reshape(stage_a.shape).astype(F32)
     values_v, gate_one, gate_two = late(0), late(1), late(2)
     grad_out = early(4 * quota)
@@ -379,7 +412,7 @@
     give_early(1)
 
     def take(a):
-        wait_bytes(g_recv.at[a], g_sems.at[a])
+        arrive("g", a)
         stage_c[...] = g_recv[a].reshape(stage_c.shape).astype(F32)
         for q in range(quota):
             for tb in range(4):
@@ -387,7 +420,9 @@
                     pl.ds(q * 4 + tb, chips, stride=rows_c), :
                 ]
         grad[a] = turned_ref[...].T.astype(BF16).reshape(2, tokens, LANES)
-        send(grad.at[a, 1 - core], grad_in.at[a], sems.at[13], c_sems.at[a], partner, group)
+        send(grad.at[a, 1 - core], grad_in.at[a], cs_sems.at[a], c_sems.at[a], partner, group)
+        expect(("grad", a), grad_in.at[a], c_sems.at[a])
+        expect(("grad out", a), grad_in.at[a], cs_sems.at[a])
 
     def give_w(a):
         block = grad[a].reshape(2 * tokens, LANES)
@@ -409,6 +444,8 @@
 
         lax.fori_loop(1, 2 * plane, one, 0)
         pltpu.make_async_copy(w_send.at[a, xx, :, y * 2 + core], w_in.at[a, here], w_sems.at[a]).start()
+        expect(("sum", a), w_in.at[a], w_sems.at[a])
+        expect(("sum out", a), w_in.at[a, pl.ds(0, 2 * plane - 1)], ws_sems.at[a])
 
     def both(arrays, c):
         left = jnp.concatenate([part for a in arrays for part in (grad[a, core], grad_in[a])], axis=1)
@@ -420,13 +457,13 @@
     give_w(1)
     take(0)
     give_w(0)
-    wait_bytes(w_other, sems.at[8])
+    arrive("other")
     for a in (1, 0):
-        wait_bytes(grad_in.at[a], c_sems.at[a])
+        arrive("grad", a)
     for c in range(groups):
         u_acc[c] = both((1, 0), c)
     take(2)
-    wait_bytes(grad_in.at[2], c_sems.at[2])
+    arrive("grad", 2)
     for c in range(groups):
         value = u_acc[c] + both((2,), c)
         u_acc[c] = value
@@ -434,12 +471,17 @@
     for step in far + near:
         other = lax.rem(group + step, groups)
         send(u_send.at[other], u_recv.at[group], sems.at[14], u_sems.at[group], me, other)
+    for step in range(1, groups):
+        other = lax.rem(group + groups - step, groups)
+        expect(("u", step), u_recv.at[other], u_sems.at[other])
+    if groups > 1:
+        expect(("u out",), u_recv.at[pl.ds(0, groups - 1)], sems.at[14])
     give_w(2)
     u_own[...] = u_acc[group]
 
     z_device = z_first + core
     for a in (1, 0, 2):
-        wait_bytes(w_in.at[a], w_sems.at[a])
+        arrive("sum", a)
         for half in range(2):
             own = w_in[a, half, zl].astype(F32)
             away = w_in[a, half, 1 - zl].astype(F32)
@@ -448,30 +490,12 @@
                 away = away + w_in[a, 2 * p + half, 1 - zl].astype(F32)
             w_own[a, half] = own
             w_relay[a, half] = away
-        send(w_relay.at[a], w_far.at[a], sems.at[15], sems.at[16], z_device, group)
-
-    wait_bytes(b_back.at[0], b_sems.at[0])
-    wait_bytes(b_back.at[1], b_sems.at[1])
-    for step in near + far:
-        other = lax.rem(group + groups - step, groups)
-        wait_bytes(u_recv.at[other], u_sems.at[other])
-    wait_bytes(w_far, sems.at[16])
-    wait_bytes(wg.at[pl.ds(0, 2 * plane + 1)], sems.at[0])
-    wait_bytes(xg.at[0], sems.at[2])
-    wait_bytes(wg.at[pl.ds(0, 2 * plane - 2)], sems.at[4])
-    if groups > 1:
-        wait_bytes(xg.at[0, pl.ds(0, groups - 1)], sems.at[6])
-        wait_bytes(u_recv.at[pl.ds(0, groups - 1)], sems.at[14])
-    wait_bytes(wg, sems.at[7])
-    wait_bytes(b_recv.at[pl.ds(0, n - 1)], sems.at[9])
-    wait_bytes(a_recv.at[pl.ds(0, chips - 1)], sems.at[11])
-    wait_bytes(grad_in, sems.at[13])
-    wait_bytes(w_far, sems.at[15])
-    for a in range(3):
-        wait_bytes(g_recv.at[a, pl.ds(0, chips - 1)], gs_sems.at[a])
-        wait_bytes(w_in.at[a, pl.ds(0, 2 * plane - 1)], ws_sems.at[a])
-    for k in range(2):
-        wait_bytes(b_back.at[k, pl.ds(0, n - 1)], bs_sems.at[k])
+        send(w_relay.at[a], w_far.at[a], ws_sems.at[3 + a], w_sems.at[3 + a], z_device, group)
+        expect(("far", a), w_far.at[a], w_sems.at[3 + a])
+        expect(("far out", a), w_far.at[a], ws_sems.at[3 + a])
+
+    for key in list(pending):
+        arrive(*key)
 
 
 def finish_kernel(
@@ -513,7 +537,7 @@
     gu_ref[...] = total.astype(BF16)
     for a in range(3):
         for half in range(2):
-            gw_ref[:, a, half * LANES : (half + 1) * LANES] = w_own[a, half] + w_far[a, half]
+            gw_ref[a, :, half * LANES : (half + 1) * LANES] = w_own[a, half] + w_far[a, half]
 
 
 def on_device(layer_input, w_in, filters, bias, cotangent):
@@ -536,7 +560,6 @@
     limit = 58 * 1024 * 1024
     spec = pltpu.VMEM((quota * blocks, 2 * LANES), F32)
 
-    w_halves = w_in.reshape(rows, 3, 2, LANES).transpose(2, 0, 1, 3).reshape(2, rows, cols)
     landed = pl.pallas_call(
         functools.partial(layer_kernel, n, groups),
         out_shape=(
@@ -549,6 +572,7 @@
         in_specs=[vmem] * 4 + [smem] + [vmem] * 6,
         out_specs=(vmem,) * 5,
         scratch_shapes=[
+            pltpu.VMEM((2, rows, cols), BF16),
             pltpu.VMEM((n, rows, cols), BF16),
             pltpu.VMEM((n, rows, cols), BF16),
             pltpu.VMEM((2, groups, tokens, width), BF16),
@@ -575,22 +599,22 @@
             pltpu.VMEM((groups, tokens, width), F32),
             pltpu.VMEM((groups, tokens, width), BF16),
             dma((17,)),
-            dma((groups,)), dma((groups,)), dma((groups,)),
-            dma((3,)), dma((3,)), dma((3,)), dma((3,)), dma((3,)),
-            dma((2,)), dma((2,)),
+            dma((groups,)), dma((groups,)), dma((groups,)), dma((groups,)),
+            dma((3,)), dma((3,)), dma((3,)), dma((3,)),
+            dma((2,)), dma((2,)), dma((6,)), dma((6,)),
         ],
         compiler_params=pltpu.CompilerParams(
             collective_id=0, has_side_effects=True, vmem_limit_bytes=limit
         ),
         name="layer",
-    )(layer_input, w_halves, filters, cotangent, bias, *(jnp.asarray(table) for table in tables(blocks)))
-
-    return pl.pallas_call(
+    )(layer_input, w_in.transpose(1, 0, 2), filters, cotangent, bias, *(jnp.asarray(table) for table in tables(blocks)))
+
+    out, grad_u, grad_w, grad_f, grad_b = pl.pallas_call(
         functools.partial(finish_kernel, n, groups),
         out_shape=(
             sds((tokens, width), BF16),
             sds((tokens, width), BF16),
-            sds((rows, 3, width), F32),
+            sds((3, rows, width), F32),
             sds((2, tokens, width), F32),
             sds((2, width), F32),
         ),
@@ -600,9 +624,10 @@
             pltpu.VMEM((2, n * rows_c, LANES), F32),
             pltpu.VMEM((2 * LANES, tokens), F32),
         ],
-        compiler_params=pltpu.CompilerParams(vmem_limit_bytes=limit // 4),
+        compiler_params=pltpu.CompilerParams(vmem_limit_bytes=limit),
         name="finish",
     )(*landed)
+    return (out, grad_u, grad_w.transpose(1, 0, 2), grad_f, grad_b)
 
 
 def solution(mesh):

time: 86.8 us -> 81.2 us (0.935)
  local copies, waits for them, and re-layouts: 6.66 us -> 0 us
  Pallas kernels: 79.1 us -> 80.5 us
    unnamed x10 -> x0, local copies, waits for them, and re-layouts: 4.62 us -> none
    reshape x3 -> x0, local copies, waits for them, and re-layouts: 1.41 us -> none  [on_device(): w_in.reshape(rows, 3, 2, LANES).transpose(2, 0, 1, 3).reshape(2, rows, cols)]
    pallas_call x1, Pallas kernels: 1.62 us -> 2.81 us  [on_device(): pl.pallas_call(functools.partial(finish_kernel, n, groups), out_shape=(sd...]
where the time goes in v3:
time: 81.2 us; the launch traced here: 81.1 us
  Pallas kernels  80.5 us (99%)
    pallas_call x1, Pallas kernels, on_device(): pl.pallas_call(functools.partial(layer_kernel, n, groups), out_shape=(sds...  77.7 us
    pallas_call x1, Pallas kernels, on_device(): pl.pallas_call(functools.partial(finish_kernel, n, groups), out_shape=(sd...  2.81 us

profile of v3, /device:TPU:1, one launch (start us, length us, event | category | flops | bytes accessed | tf_op | source)
XLA Modules:
  0.0 81.1 jit_solution(14459660523009524716)
XLA Ops:
  0.6 77.7 %layer.1 = (bf16[2,64,16,128]{3,2,1,0:T(8,128)(2,1)}, f32[3,2,16,128]{3,2,1,0:T(8,128)}, f32[3,2,16,128]{3,2,1,0:T(8,128)}, f32[256,256]{1,0:T(8,128)}, bf16[4,256,256]{2,1,0:T(8,128)(2,1)}) custom-call(bf16[256,256]{1,0:T(8,128)(2,1)} %x_ref.1, bf16[3,16,256]{2,1,0:T(8,128)(2,1)} %bitcast.2, f32[2,256,256]{2,1,0:T(8,128)} %filters_ref.1, ...), custom_call_target="tpu_custom_call" | custom-call | tf_op jit(solution)/shard_map/layer/pallas_call | solution.py:563
  78.3 2.8 %finish.1 = (bf16[256,256]{1,0:T(8,128)(2,1)}, bf16[256,256]{1,0:T(8,128)(2,1)}, f32[3,16,256]{2,1,0:T(8,128)}, f32[2,256,256]{2,1,0:T(8,128)}, f32[2,256]{1,0:T(2,128)}) custom-call(bf16[2,64,16,128]{3,2,1,0:T(8,128)(2,1)} %get-tuple-element.15.b_back, f32[3,2,16,128]{3,2,1,0:T(8,128)} %get-tuple-element.16.w_own, ...), custom_call_target="tpu_custom_call" | custom-call | tf_op jit(solution)/shard_map/finish/pallas_call | solution.py:612

commit v4 on v3

--- a/solution.py
+++ b/solution.py
@@ -84,14 +84,15 @@
 
 
 def layer_kernel(
-    n, groups, x_ref, w_in_ref, filters_ref, cot_ref, bias_ref,
-    first_ref, middle_ref, middle_t_ref, last_ref, cos_ref, sin_ref,
-    b_back, w_own, w_far, u_own, u_recv,
+    n, groups, x_ref, w_in_ref, bias_ref, filters_at, cot_at,
+    first_at, middle_at, middle_t_at, last_at, cos_at, sin_at,
+    b_back, w_own, w_far, u_own,
+    filters_ref, cot_ref, first_ref, middle_ref, middle_t_ref, last_ref, cos_ref, sin_ref, load_sems,
     w_ref, wg, w_other, xg, xt, total, stage_a, a_send, a_recv, stage_b, b_send, b_recv,
     spec_h1, spec_h2, spec_v, spec_z, spec_g1, spec_g2,
     stage_c, g_send, g_recv, stage_d, b_give, turned_ref, grad, grad_in,
-    w_send, w_in, w_relay, u_acc, u_send,
-    sems, x_sems, xp_sems, xr_sems, u_sems, gs_sems, g_sems, cs_sems, c_sems, bs_sems, b_sems, ws_sems, w_sems,
+    w_send, w_in, w_relay, u_acc, u_send, u_in, u_far,
+    sems, x_sems, xs_sems, xp_sems, xr_sems, u_sems, us_sems, gs_sems, g_sems, cs_sems, c_sems, bs_sems, b_sems, ws_sems, w_sems,
 ):
     me = lax.axis_index("seq")
     group = lax.axis_index("chan")
@@ -127,6 +128,15 @@
 
     barrier = greet(me, n, group, groups)
 
+    for k, (here_ref, there_ref) in enumerate(
+        (
+            (filters_ref, filters_at), (cot_ref, cot_at), (first_ref, first_at), (middle_ref, middle_at),
+            (middle_t_ref, middle_t_at), (last_ref, last_at), (cos_ref, cos_at), (sin_ref, sin_at),
+        )
+    ):
+        pltpu.make_async_copy(there_ref, here_ref, load_sems.at[k]).start()
+        expect(("load", k), here_ref, load_sems.at[k])
+
     for half in range(2):
         for a in range(3):
             w_ref[half, :, a * LANES : (a + 1) * LANES] = w_in_ref[a, :, half * LANES : (half + 1) * LANES]
@@ -141,25 +151,35 @@
                         top : top + chips, tb * LANES : (tb + 1) * LANES
                     ]
 
-    spread(filters_ref[0], 0)
-    spread(filters_ref[1], 2 * quota)
-    spread(cot_ref[...].astype(F32), 4 * quota)
-    for peer in range(n):
-        stage_b[pl.ds(peer * rows_b + 6 * quota, 2 * quota), :] = jnp.zeros((2 * quota, LANES), F32)
-    b_send[...] = stage_b[...].astype(BF16).reshape(b_send.shape)
     xg[core, group] = x_ref[...]
     pl.semaphore_wait(barrier, n - 1 + groups - 1)
 
-    near = [step for step in range(1, groups) if min(step, groups - step) == 1]
-    far = [step for step in range(1, groups) if min(step, groups - step) > 1]
-    for step in far + near:
-        send(x_ref, xg.at[core, group], sems.at[2], x_sems.at[group], me, lax.rem(group + step, groups))
-    for step in range(1, groups):
-        other = lax.rem(group + groups - step, groups)
-        expect(("x", step), xg.at[core, other], x_sems.at[other])
     z_first = in_plane(xx * ny + y, 0, 1 - zl)
     for c in range(2):
         send(w_ref.at[c], wg.at[me], sems.at[0], sems.at[3], z_first + c, group)
+
+    part = tokens // 2
+    after, before, across = (lax.rem(group + step, groups) for step in (1, 3, 2))
+
+    def half_x(side, source, half):
+        return xg.at[side, source, pl.ds(half * part, part)]
+
+    def send_x(half, target, k):
+        own = half_x(core, group, half)
+        send(own, own, xs_sems.at[k], x_sems.at[2 * group + half], me, target)
+        expect(("x out", k), own, xs_sems.at[k])
+
+    def relay_x(source, half, k):
+        ref = half_x(core, source, half)
+        send(ref, ref, xr_sems.at[k], xp_sems.at[2 * source + half], partner, group)
+        expect(("xp", k), half_x(1 - core, source, half), xp_sems.at[2 * source + half])
+        expect(("x relay", k), ref, xr_sems.at[k])
+
+    for k, (half, target) in enumerate(((0, after), (1, before), (1, after), (0, before))):
+        send_x(half, target, k)
+    arrivals = ((before, 0), (after, 1), (before, 1), (after, 0), (across, 0), (across, 1))
+    for k, (source, half) in enumerate(arrivals):
+        expect(("x", k), half_x(core, source, half), x_sems.at[2 * source + half])
 
     def send_w(step, carry):
         peer = lax.rem(here + step, 2 * plane)
@@ -169,38 +189,36 @@
 
     lax.fori_loop(1, 2 * plane, send_w, 0)
     pltpu.make_async_copy(w_ref.at[core], wg.at[me], sems.at[1]).start()
-    send(x_ref, xg.at[core, group], sems.at[2], xp_sems.at[group], partner, group)
-    expect(("x out",), xg.at[0], sems.at[2])
     expect(("w",), wg.at[pl.ds(0, 2 * plane)], sems.at[1])
     expect(("w out",), wg.at[pl.ds(0, 2 * plane + 1)], sems.at[0])
-    expect(("xp", 0), xg.at[1 - core, group], xp_sems.at[group])
+    for half in range(2):
+        relay_x(group, half, 6 + half)
+
+    arrive("load", 0)
+    spread(filters_ref[0], 0)
     wait_bytes(wg.at[pl.ds(z_first, 2)], sems.at[3])
 
     def forward_w(step, carry):
         p = lax.rem(here // 2 + step, plane)
-        part = wg.at[pl.ds(z_first, 2)]
-        send(part, part, sems.at[4], sems.at[5], in_plane(p, core, zl), group)
+        pair = wg.at[pl.ds(z_first, 2)]
+        send(pair, pair, sems.at[4], sems.at[5], in_plane(p, core, zl), group)
         return carry
 
     lax.fori_loop(1, plane, forward_w, 0)
     expect(("w rest",), wg.at[pl.ds(0, 2 * plane - 2)], sems.at[5])
     expect(("w rest out",), wg.at[pl.ds(0, 2 * plane - 2)], sems.at[4])
-
-    def relay(step):
-        other = lax.rem(group + groups - step, groups)
-        arrive("x", step)
-        part = xg.at[core, other]
-        send(part, part, xr_sems.at[step], xp_sems.at[other], partner, group)
-        expect(("xp", step), xg.at[1 - core, other], xp_sems.at[other])
-        expect(("x relay", step), xg.at[1 - core, other], xr_sems.at[step])
-
-    for step in near:
-        relay(step)
-    arrive("w")
-    arrive("w rest")
-    send(wg, w_other, sems.at[7], sems.at[8], partner, group)
-    expect(("other",), w_other, sems.at[8])
-    expect(("other out",), w_other, sems.at[7])
+    spread(filters_ref[1], 2 * quota)
+    for k in range(2):
+        arrive("x", k)
+        source, half = arrivals[k]
+        ref = half_x(core, source, half)
+        send(ref, ref, xs_sems.at[4 + k], x_sems.at[2 * source + half], me, after if k == 0 else before)
+        expect(("x out", 4 + k), ref, xs_sems.at[4 + k])
+        relay_x(source, half, k)
+    arrive("load", 1)
+    spread(cot_ref[...].astype(F32), 4 * quota)
+    for peer in range(n):
+        b_send[peer] = stage_b[peer * rows_b : (peer + 1) * rows_b, :].astype(BF16)
 
     def give_b(step, carry):
         peer = lax.rem(me + step, n)
@@ -211,27 +229,37 @@
     pltpu.make_async_copy(b_send.at[me], b_recv.at[me], sems.at[10]).start()
     expect(("b",), b_recv, sems.at[10])
     expect(("b out",), b_recv.at[pl.ds(0, n - 1)], sems.at[9])
+    for k in (2, 3):
+        arrive("x", k)
+        relay_x(*arrivals[k], k)
+    arrive("w")
+    arrive("w rest")
 
     def weights(ref, c):
         return ref[pl.ds(c * slots, slots)].reshape(depth, cols)
 
-    def project(side, step):
-        other = lax.rem(group + groups - step, groups)
-        if side == 1:
-            arrive("xp", step)
+    def project(side, source, first=False):
         at = core if side == 0 else 1 - core
-        term = matmul(xg[at, other], weights(wg, other))
-        total[at] = term if step == 0 else total[at] + term
-
-    for step in [0] + near:
-        project(0, step)
-    for step in [0] + near:
-        project(1, step)
-    for step in far:
-        relay(step)
-        project(0, step)
-    for step in far:
-        project(1, step)
+        term = matmul(xg[at, source], weights(wg, source))
+        total[at] = term if first else total[at] + term
+
+    project(0, group, True)
+    for k in (6, 7):
+        arrive("xp", k)
+    project(1, group, True)
+    project(0, before)
+    project(0, after)
+    for k in range(4):
+        arrive("xp", k)
+    project(1, before)
+    project(1, after)
+    for k in (4, 5):
+        arrive("x", k)
+        relay_x(*arrivals[k], k)
+    project(0, across)
+    for k in (4, 5):
+        arrive("xp", k)
+    project(1, across)
     turned = total[...].reshape(2 * tokens, cols).T
     for a in range(3):
         for q in range(quota):
@@ -251,6 +279,11 @@
     pltpu.make_async_copy(a_send.at[chip], a_recv.at[chip], sems.at[12]).start()
     expect(("a",), a_recv, sems.at[12])
     expect(("a out",), a_recv.at[pl.ds(0, chips - 1)], sems.at[11])
+    send(wg, w_other, sems.at[7], sems.at[8], partner, group)
+    expect(("other",), w_other, sems.at[8])
+    expect(("other out",), w_other, sems.at[7])
+    for k in range(2, 8):
+        arrive("load", k)
 
     def columns(ref, start, stride):
         return jnp.concatenate(
@@ -380,7 +413,8 @@
         expect(("back out", k), b_back.at[k, pl.ds(0, n - 1)], bs_sems.at[k])
 
     arrive("b")
-    stage_b[...] = b_recv[...].reshape(stage_b.shape).astype(F32)
+    for peer in range(n):
+        stage_b[peer * rows_b : (peer + 1) * rows_b, :] = b_recv[peer].astype(F32)
     forward(early(0), spec_h1, True)
     forward(early(2 * quota), spec_h2, True)
     for c in range(groups):
@@ -390,18 +424,19 @@
     values_v, gate_one, gate_two = late(0), late(1), late(2)
     grad_out = early(4 * quota)
     skip_one, skip_two = skip(0), skip(1)
+    grad_conv_two = grad_out * gate_two
+    forward(grad_conv_two, spec_g2)
     forward(values_v, spec_v, True)
+    grad_mixed = backward(spec_h2, spec_g2, True, False) + skip_two * grad_conv_two
     conv_one = backward(spec_h1, spec_v, False, False) + skip_one * values_v
     mixed = gate_one * conv_one
-    grad_conv_two = grad_out * gate_two
-    forward(grad_conv_two, spec_g2)
-    grad_mixed = backward(spec_h2, spec_g2, True, False) + skip_two * grad_conv_two
+    grad_conv_one = grad_mixed * gate_one
     give_late(grad_mixed * conv_one, 1)
-    grad_conv_one = grad_mixed * gate_one
     forward(grad_conv_one, spec_g1)
-    give_late(backward(spec_h1, spec_g1, True, False) + skip_one * grad_conv_one, 0)
     forward(mixed, spec_z)
+    grad_v = backward(spec_h1, spec_g1, True, False) + skip_one * grad_conv_one
     conv_two = backward(spec_h2, spec_z, False, False) + skip_two * mixed
+    give_late(grad_v, 0)
     give_late(grad_out * conv_two, 2)
     put_early(gate_two * conv_two, 0)
     put_early(backward(spec_g2, spec_z, False, True), 2 * quota)
@@ -426,7 +461,6 @@
 
     def give_w(a):
         block = grad[a].reshape(2 * tokens, LANES)
-        per = n // groups
         for c in range(groups):
             term = matmul(xt[c], block).astype(BF16).reshape(slots, depth // slots, LANES)
             for k in range(slots):
@@ -464,20 +498,35 @@
         u_acc[c] = both((1, 0), c)
     take(2)
     arrive("grad", 2)
-    for c in range(groups):
-        value = u_acc[c] + both((2,), c)
-        u_acc[c] = value
-        u_send[c] = value.astype(BF16)
-    for step in far + near:
-        other = lax.rem(group + step, groups)
-        send(u_send.at[other], u_recv.at[group], sems.at[14], u_sems.at[group], me, other)
-    for step in range(1, groups):
-        other = lax.rem(group + groups - step, groups)
-        expect(("u", step), u_recv.at[other], u_sems.at[other])
-    if groups > 1:
-        expect(("u out",), u_recv.at[pl.ds(0, groups - 1)], sems.at[14])
+
+    def send_u(ref, slot, target):
+        send(ref, u_in.at[slot], us_sems.at[slot], u_sems.at[slot], me, target)
+        expect(("u", slot), u_in.at[slot], u_sems.at[slot])
+        expect(("u out", slot), u_in.at[slot], us_sems.at[slot])
+
+    def half_u(dest, half):
+        return u_send.at[dest, pl.ds(half * part, part)]
+
+    def finish_u(dest):
+        value = u_acc[dest] + both((2,), dest)
+        u_acc[dest] = value
+        u_send[dest] = value.astype(BF16)
+
+    finish_u(across)
+    send_u(half_u(across, 0), 0, after)
+    send_u(half_u(across, 1), 1, before)
+    finish_u(after)
+    send_u(half_u(after, 1), 2, after)
+    finish_u(before)
+    send_u(half_u(before, 0), 3, before)
+    u_own[...] = u_acc[group] + both((2,), group)
     give_w(2)
-    u_own[...] = u_acc[group]
+    arrive("u", 0)
+    u_far[0] = (u_acc[after, :part] + u_in[0].astype(F32)).astype(BF16)
+    send_u(u_far.at[0], 4, after)
+    arrive("u", 1)
+    u_far[1] = (u_acc[before, part:] + u_in[1].astype(F32)).astype(BF16)
+    send_u(u_far.at[1], 5, before)
 
     z_device = z_first + core
     for a in (1, 0, 2):
@@ -494,14 +543,17 @@
         expect(("far", a), w_far.at[a], w_sems.at[3 + a])
         expect(("far out", a), w_far.at[a], ws_sems.at[3 + a])
 
+    for slot in range(2, 6):
+        arrive("u", slot)
+    u_own[:part] = u_own[:part] + u_in[3].astype(F32) + u_in[4].astype(F32)
+    u_own[part:] = u_own[part:] + u_in[2].astype(F32) + u_in[5].astype(F32)
     for key in list(pending):
         arrive(*key)
 
 
 def finish_kernel(
-    n, groups, b_back, w_own, w_far, u_own, u_recv, out_ref, gu_ref, gw_ref, gf_ref, gb_ref, stage, turned_ref
+    n, b_back, w_own, w_far, u_own, out_ref, gu_ref, gw_ref, gf_ref, gb_ref, stage, turned_ref
 ):
-    group = lax.axis_index("chan")
     chips = n // 2
     quota = LANES // chips
     rows_c = 4 * quota
@@ -531,10 +583,7 @@
                 moved = full if q == 0 else pltpu.roll(full, q * chips, 1)
                 line = jnp.where((lane >= q * chips) & (lane < (q + 1) * chips), moved, line)
             gb_ref[f : f + 1, half * LANES : (half + 1) * LANES] = line
-    total = u_own[...]
-    for step in range(1, groups):
-        total = total + u_recv[lax.rem(group + step, groups)].astype(F32)
-    gu_ref[...] = total.astype(BF16)
+    gu_ref[...] = u_own[...].astype(BF16)
     for a in range(3):
         for half in range(2):
             gw_ref[a, :, half * LANES : (half + 1) * LANES] = w_own[a, half] + w_far[a, half]
@@ -551,7 +600,7 @@
     plane = nx * ny
     quota = LANES // chips
     blocks = 4 * chips
-    rows_a, rows_b, rows_c = 12 * quota, 8 * quota, 4 * quota
+    rows_a, rows_b, rows_c = 12 * quota, 6 * quota, 4 * quota
     cols = 3 * LANES
     vmem = pl.BlockSpec(memory_space=pltpu.VMEM)
     smem = pl.BlockSpec(memory_space=pltpu.SMEM)
@@ -560,6 +609,7 @@
     limit = 58 * 1024 * 1024
     spec = pltpu.VMEM((quota * blocks, 2 * LANES), F32)
 
+    constants = [jnp.asarray(table) for table in tables(blocks)]
     landed = pl.pallas_call(
         functools.partial(layer_kernel, n, groups),
         out_shape=(
@@ -567,11 +617,12 @@
             sds((3, 2, rows, LANES), F32),
             sds((3, 2, rows, LANES), F32),
             sds((tokens, width), F32),
-            sds((groups, tokens, width), BF16),
         ),
-        in_specs=[vmem] * 4 + [smem] + [vmem] * 6,
-        out_specs=(vmem,) * 5,
+        in_specs=[vmem, vmem, smem] + [pl.BlockSpec(memory_space=pl.ANY)] * 8,
+        out_specs=(vmem,) * 4,
         scratch_shapes=[
+            *(pltpu.VMEM(array.shape, array.dtype) for array in (filters, cotangent, *constants)),
+            dma((8,)),
             pltpu.VMEM((2, rows, cols), BF16),
             pltpu.VMEM((n, rows, cols), BF16),
             pltpu.VMEM((n, rows, cols), BF16),
@@ -598,8 +649,10 @@
             pltpu.VMEM((3, 2, rows, LANES), F32),
             pltpu.VMEM((groups, tokens, width), F32),
             pltpu.VMEM((groups, tokens, width), BF16),
+            pltpu.VMEM((6, tokens // 2, width), BF16),
+            pltpu.VMEM((2, tokens // 2, width), BF16),
             dma((17,)),
-            dma((groups,)), dma((groups,)), dma((groups,)), dma((groups,)),
+            dma((2 * groups,)), dma((6,)), dma((2 * groups,)), dma((8,)), dma((6,)), dma((6,)),
             dma((3,)), dma((3,)), dma((3,)), dma((3,)),
             dma((2,)), dma((2,)), dma((6,)), dma((6,)),
         ],
@@ -607,10 +660,10 @@
             collective_id=0, has_side_effects=True, vmem_limit_bytes=limit
         ),
         name="layer",
-    )(layer_input, w_in.transpose(1, 0, 2), filters, cotangent, bias, *(jnp.asarray(table) for table in tables(blocks)))
+    )(layer_input, w_in.transpose(1, 0, 2), bias, filters, cotangent, *constants)
 
     out, grad_u, grad_w, grad_f, grad_b = pl.pallas_call(
-        functools.partial(finish_kernel, n, groups),
+        functools.partial(finish_kernel, n),
         out_shape=(
             sds((tokens, width), BF16),
             sds((tokens, width), BF16),
@@ -618,7 +671,7 @@
             sds((2, tokens, width), F32),
             sds((2, width), F32),
         ),
-        in_specs=[vmem] * 5,
+        in_specs=[vmem] * 4,
         out_specs=(vmem,) * 5,
         scratch_shapes=[
             pltpu.VMEM((2, n * rows_c, LANES), F32),

time: 81.2 us -> 68.4 us (0.84)
  Pallas kernels: 80.5 us -> 67.7 us
    pallas_call x1, Pallas kernels: 77.7 us -> 65.1 us  [on_device(): pl.pallas_call(functools.partial(layer_kernel, n, groups), out_shape=(sds...]
where the time goes in v4:
time: 68.4 us; the launch traced here: 68.3 us
  Pallas kernels  67.7 us (99%)
    pallas_call x1, Pallas kernels, on_device(): pl.pallas_call(functools.partial(layer_kernel, n, groups), out_shape=(sds...  65.1 us
    pallas_call x1, Pallas kernels, on_device(): pl.pallas_call(functools.partial(finish_kernel, n), out_shape=(sds((token...  2.6 us

profile of v4, /device:TPU:1, one launch (start us, length us, event | category | flops | bytes accessed | tf_op | source)
XLA Modules:
  0.0 68.3 jit_solution(9083258305458574735)
XLA Ops:
  0.6 65.1 %layer.1 = (bf16[2,64,16,128]{3,2,1,0:T(8,128)(2,1)}, f32[3,2,16,128]{3,2,1,0:T(8,128)}, f32[3,2,16,128]{3,2,1,0:T(8,128)}, f32[256,256]{1,0:T(8,128)}) custom-call(bf16[256,256]{1,0:T(8,128)(2,1)} %x_ref.1, bf16[3,16,256]{2,1,0:T(8,128)(2,1)} %bitcast.2, f32[2,256]{1,0:T(2,128)} %bias_ref.1, f32[2,256,256]{2,1,0:T(8,128)} %filters_at.1, ...), custom_call_target="tpu_custom_call" | custom-call | tf_op jit(solution)/shard_map/layer/pallas_call | solution.py:613
  65.7 2.6 %finish.1 = (bf16[256,256]{1,0:T(8,128)(2,1)}, bf16[256,256]{1,0:T(8,128)(2,1)}, f32[3,16,256]{2,1,0:T(8,128)}, f32[2,256,256]{2,1,0:T(8,128)}, f32[2,256]{1,0:T(2,128)}) custom-call(bf16[2,64,16,128]{3,2,1,0:T(8,128)(2,1)} %get-tuple-element.14.b_back, f32[3,2,16,128]{3,2,1,0:T(8,128)} %get-tuple-element.15.w_own, ...), custom_call_target="tpu_custom_call" | custom-call | tf_op jit(solution)/shard_map/finish/pallas_call | solution.py:665

commit v5 on v4

--- a/solution.py
+++ b/solution.py
@@ -33,7 +33,7 @@
     def parts(table, axis):
         high = table.astype(ml_dtypes.bfloat16)
         low = (table - high.astype(np.float64)).astype(ml_dtypes.bfloat16)
-        return np.concatenate([high, low, high], axis=axis)
+        return np.concatenate([high, low], axis=axis)
 
     return (
         parts(first, 1),
@@ -47,12 +47,6 @@
 
 def matmul(left, right, dims=((1,), (0,))):
     return lax.dot_general(left, right, (dims, ((), ())), preferred_element_type=F32)
-
-
-def split(value):
-    high = value.astype(BF16)
-    low = (value - high.astype(F32)).astype(BF16)
-    return high, low
 
 
 def greet(me, peers, group, groups):
@@ -92,7 +86,7 @@
     spec_h1, spec_h2, spec_v, spec_z, spec_g1, spec_g2,
     stage_c, g_send, g_recv, stage_d, b_give, turned_ref, grad, grad_in,
     w_send, w_in, w_relay, u_acc, u_send, u_in, u_far,
-    sems, x_sems, xs_sems, xp_sems, xr_sems, u_sems, us_sems, gs_sems, g_sems, cs_sems, c_sems, bs_sems, b_sems, ws_sems, w_sems,
+    sems, x_sems, xs_sems, xp_sems, xr_sems, u_sems, us_sems, gs_sems, g_sems, cs_sems, c_sems, ws_sems, w_sems,
 ):
     me = lax.axis_index("seq")
     group = lax.axis_index("chan")
@@ -110,7 +104,7 @@
     quota = LANES // chips
     blocks = 4 * chips
     rows_a, rows_b = a_send.shape[1], b_send.shape[1]
-    rows_c = 4 * quota
+    rows_c, rows_d = 4 * quota, 8 * quota
     tokens, depth = x_ref.shape
     cols = wg.shape[2]
     slots = depth // wg.shape[1]
@@ -256,18 +250,23 @@
     for k in (4, 5):
         arrive("x", k)
         relay_x(*arrivals[k], k)
+    def lay_out(at):
+        turned = total[at].T
+        for a in range(3):
+            for q in range(quota):
+                top = a * LANES + q * chips
+                for tb in range(2):
+                    row = (a * quota + q) * 4 + 2 * at + tb
+                    stage_a[pl.ds(row, chips, stride=rows_a), :] = turned[
+                        top : top + chips, tb * LANES : (tb + 1) * LANES
+                    ]
+
     project(0, across)
+    lay_out(core)
     for k in (4, 5):
         arrive("xp", k)
     project(1, across)
-    turned = total[...].reshape(2 * tokens, cols).T
-    for a in range(3):
-        for q in range(quota):
-            top = a * LANES + q * chips
-            for tb in range(4):
-                stage_a[pl.ds((a * quota + q) * 4 + tb, chips, stride=rows_a), :] = turned[
-                    top : top + chips, tb * LANES : (tb + 1) * LANES
-                ]
+    lay_out(1 - core)
     a_send[...] = stage_a[...].astype(BF16).reshape(a_send.shape)
 
     def give_a(step, carry):
@@ -305,26 +304,22 @@
     def piece(value, q):
         return value[:, q * LANES : (q + 1) * LANES]
 
-    def forward(value, spec, exact=False):
-        high, low = split(value)
-        if exact:
-            wide = matmul(first_ref[:, : 2 * blocks], jnp.concatenate([high, high], axis=0))
-        else:
-            wide = matmul(first_ref[...], jnp.concatenate([high, high, low], axis=0))
+    def twice(value, axis):
+        high = value.astype(BF16)
+        return jnp.concatenate([high, high], axis=axis)
+
+    def forward(value, spec):
+        wide = matmul(first_ref[...], twice(value, 0))
         turn_cos, turn_sin = cos_ref[...], sin_ref[...]
         for q in range(quota):
             re = piece(wide[:blocks], q)
             im = piece(wide[blocks:], q)
-            high, low = split(
-                jnp.concatenate([re * turn_cos + im * turn_sin, im * turn_cos - re * turn_sin], axis=1)
-            )
-            spec[q * blocks : (q + 1) * blocks, :] = matmul(
-                jnp.concatenate([high, high, low], axis=1), middle_ref[...]
-            )
+            turned = jnp.concatenate([re * turn_cos + im * turn_sin, im * turn_cos - re * turn_sin], axis=1)
+            spec[q * blocks : (q + 1) * blocks, :] = matmul(twice(turned, 1), middle_ref[...])
 
     def backward(left, right, conj_left, conj_right):
         turn_cos, turn_sin = cos_ref[...], sin_ref[...]
-        columns_high, columns_low = [], []
+        parts = []
         for q in range(quota):
             rows = slice(q * blocks, (q + 1) * blocks)
             l_re, l_im = left[rows, :LANES], left[rows, LANES:]
@@ -337,17 +332,10 @@
                 y_im = l_im * r_re - l_re * r_im
             else:
                 y_im = l_re * r_im + l_im * r_re
-            high, low = split(jnp.concatenate([y_re, y_im], axis=1))
-            out = matmul(jnp.concatenate([high, high, low], axis=1), middle_t_ref[...])
+            out = matmul(twice(jnp.concatenate([y_re, y_im], axis=1), 1), middle_t_ref[...])
             re, im = out[:, :LANES], out[:, LANES:]
-            high, low = split(
-                jnp.concatenate([re * turn_cos - im * turn_sin, im * turn_cos + re * turn_sin], axis=0)
-            )
-            columns_high.append(high)
-            columns_low.append(low)
-        high = jnp.concatenate(columns_high, axis=1)
-        low = jnp.concatenate(columns_low, axis=1)
-        return matmul(last_ref[...], jnp.concatenate([high, high, low], axis=0))
+            parts.append(jnp.concatenate([re * turn_cos - im * turn_sin, im * turn_cos + re * turn_sin], axis=0))
+        return matmul(last_ref[...], twice(jnp.concatenate(parts, axis=1), 0))
 
     def skip(f):
         return jnp.concatenate(
@@ -358,29 +346,32 @@
             axis=1,
         )
 
-    def give_late(value, a):
+    order = {1: 0, 0: 1, 2: 2}
+
+    def put_late(value, a):
         for q in range(quota):
             for tb in range(4):
                 stage_c[pl.ds(q * 4 + tb, chips, stride=rows_c), :] = piece(value, q)[
                     tb * chips : (tb + 1) * chips
                 ]
-        g_send[a] = stage_c[...].astype(BF16).reshape(chips, rows_c, LANES)
-
+        g_send[:, order[a]] = stage_c[...].astype(BF16).reshape(chips, rows_c, LANES)
+
+    def give_late(k, span):
         def one(step, carry):
             peer = lax.rem(chip + step, chips)
-            send(g_send.at[a, peer], g_recv.at[a, chip], gs_sems.at[a], g_sems.at[a], 2 * peer + core, group)
+            send(g_send.at[peer, span], g_recv.at[chip, span], gs_sems.at[k], g_sems.at[k], 2 * peer + core, group)
             return carry
 
         lax.fori_loop(1, chips, one, 0)
-        pltpu.make_async_copy(g_send.at[a, chip], g_recv.at[a, chip], g_sems.at[a]).start()
-        expect(("g", a), g_recv.at[a], g_sems.at[a])
-        expect(("g out", a), g_recv.at[a, pl.ds(0, chips - 1)], gs_sems.at[a])
+        pltpu.make_async_copy(g_send.at[chip, span], g_recv.at[chip, span], g_sems.at[k]).start()
+        expect(("g", k), g_recv.at[:, span], g_sems.at[k])
+        expect(("g out", k), g_recv.at[pl.ds(0, chips - 1), span], gs_sems.at[k])
 
     def put_early(value, base):
         for q in range(quota):
             for tb in range(4):
-                at = (tb // 2) * rows_c + base + q * 2 + tb % 2
-                stage_d[pl.ds(at, chips, stride=2 * rows_c), :] = piece(value, q)[
+                at = (tb // 2) * rows_d + base + q * 2 + tb % 2
+                stage_d[pl.ds(at, chips, stride=2 * rows_d), :] = piece(value, q)[
                     tb * chips : (tb + 1) * chips
                 ]
 
@@ -396,27 +387,28 @@
             row = jnp.where(lane == chips + chip, two, row)
             row = jnp.where(lane == 2 * chips + chip, three, row)
             for half in range(2):
-                at = half * rows_c + 2 * quota + f * quota + q
-                stage_d[pl.ds(at, chips, stride=2 * rows_c), :] = jnp.broadcast_to(row, (chips, LANES))
-
-    def give_early(k):
-        b_give[k] = stage_d[...].astype(BF16).reshape(n, rows_c, LANES)
+                at = half * rows_d + 6 * quota + f * quota + q
+                stage_d[pl.ds(at, chips, stride=2 * rows_d), :] = jnp.broadcast_to(row, (chips, LANES))
+
+    def give_early():
+        for peer in range(n):
+            b_give[peer] = stage_d[peer * rows_d : (peer + 1) * rows_d, :].astype(BF16)
 
         def one(step, carry):
             peer = lax.rem(me + step, n)
-            send(b_give.at[k, peer], b_back.at[k, me], bs_sems.at[k], b_sems.at[k], peer, group)
+            send(b_give.at[peer], b_back.at[me], sems.at[14], sems.at[15], peer, group)
             return carry
 
         lax.fori_loop(1, n, one, 0)
-        pltpu.make_async_copy(b_give.at[k, me], b_back.at[k, me], b_sems.at[k]).start()
-        expect(("back", k), b_back.at[k], b_sems.at[k])
-        expect(("back out", k), b_back.at[k, pl.ds(0, n - 1)], bs_sems.at[k])
+        pltpu.make_async_copy(b_give.at[me], b_back.at[me], sems.at[15]).start()
+        expect(("back",), b_back, sems.at[15])
+        expect(("back out",), b_back.at[pl.ds(0, n - 1)], sems.at[14])
 
     arrive("b")
     for peer in range(n):
         stage_b[peer * rows_b : (peer + 1) * rows_b, :] = b_recv[peer].astype(F32)
-    forward(early(0), spec_h1, True)
-    forward(early(2 * quota), spec_h2, True)
+    forward(early(0), spec_h1)
+    forward(early(2 * quota), spec_h2)
     for c in range(groups):
         xt[c] = xg[:, c].reshape(2 * tokens, depth).astype(F32).T.astype(BF16)
     arrive("a")
@@ -426,29 +418,29 @@
     skip_one, skip_two = skip(0), skip(1)
     grad_conv_two = grad_out * gate_two
     forward(grad_conv_two, spec_g2)
-    forward(values_v, spec_v, True)
+    forward(values_v, spec_v)
     grad_mixed = backward(spec_h2, spec_g2, True, False) + skip_two * grad_conv_two
     conv_one = backward(spec_h1, spec_v, False, False) + skip_one * values_v
     mixed = gate_one * conv_one
     grad_conv_one = grad_mixed * gate_one
-    give_late(grad_mixed * conv_one, 1)
+    put_late(grad_mixed * conv_one, 1)
+    give_late(0, pl.ds(0, 1))
     forward(grad_conv_one, spec_g1)
     forward(mixed, spec_z)
     grad_v = backward(spec_h1, spec_g1, True, False) + skip_one * grad_conv_one
     conv_two = backward(spec_h2, spec_z, False, False) + skip_two * mixed
-    give_late(grad_v, 0)
-    give_late(grad_out * conv_two, 2)
+    put_late(grad_v, 0)
+    put_late(grad_out * conv_two, 2)
+    give_late(1, pl.ds(1, 2))
     put_early(gate_two * conv_two, 0)
     put_early(backward(spec_g2, spec_z, False, True), 2 * quota)
-    give_early(0)
-    put_early(backward(spec_g1, spec_v, False, True), 0)
+    put_early(backward(spec_g1, spec_v, False, True), 4 * quota)
     put_skip(grad_conv_one * values_v, 0)
     put_skip(grad_conv_two * mixed, 1)
-    give_early(1)
+    give_early()
 
     def take(a):
-        arrive("g", a)
-        stage_c[...] = g_recv[a].reshape(stage_c.shape).astype(F32)
+        stage_c[...] = g_recv[:, order[a]].reshape(stage_c.shape).astype(F32)
         for q in range(quota):
             for tb in range(4):
                 turned_ref[q * chips : (q + 1) * chips, tb * LANES : (tb + 1) * LANES] = stage_c[
@@ -481,22 +473,26 @@
         expect(("sum", a), w_in.at[a], w_sems.at[a])
         expect(("sum out", a), w_in.at[a, pl.ds(0, 2 * plane - 1)], ws_sems.at[a])
 
-    def both(arrays, c):
-        left = jnp.concatenate([part for a in arrays for part in (grad[a, core], grad_in[a])], axis=1)
-        wide = [weights(wg, c), weights(w_other, c)]
-        right = jnp.concatenate([piece(part, a) for a in arrays for part in wide], axis=1)
-        return matmul(left, right, ((1,), (1,)))
-
+    def into_u(terms, c):
+        left, right = [], []
+        for a, own in terms:
+            left.append(grad[a, core] if own else grad_in[a])
+            right.append(piece(weights(wg if own else w_other, c), a))
+        return matmul(jnp.concatenate(left, axis=1), jnp.concatenate(right, axis=1), ((1,), (1,)))
+
+    arrive("g", 0)
     take(1)
     give_w(1)
+    arrive("other")
+    arrive("grad", 1)
+    for c in range(groups):
+        u_acc[c] = into_u(((1, True), (1, False)), c)
+    arrive("g", 1)
     take(0)
-    give_w(0)
-    arrive("other")
-    for a in (1, 0):
-        arrive("grad", a)
+    take(2)
     for c in range(groups):
-        u_acc[c] = both((1, 0), c)
-    take(2)
+        u_acc[c] = u_acc[c] + into_u(((0, True), (2, True)), c)
+    arrive("grad", 0)
     arrive("grad", 2)
 
     def send_u(ref, slot, target):
@@ -507,8 +503,11 @@
     def half_u(dest, half):
         return u_send.at[dest, pl.ds(half * part, part)]
 
+    def into_last(dest):
+        return into_u(((0, False), (2, False)), dest)
+
     def finish_u(dest):
-        value = u_acc[dest] + both((2,), dest)
+        value = u_acc[dest] + into_last(dest)
         u_acc[dest] = value
         u_send[dest] = value.astype(BF16)
 
@@ -519,14 +518,15 @@
     send_u(half_u(after, 1), 2, after)
     finish_u(before)
     send_u(half_u(before, 0), 3, before)
-    u_own[...] = u_acc[group] + both((2,), group)
-    give_w(2)
+    u_own[...] = u_acc[group] + into_last(group)
+    give_w(0)
     arrive("u", 0)
     u_far[0] = (u_acc[after, :part] + u_in[0].astype(F32)).astype(BF16)
     send_u(u_far.at[0], 4, after)
     arrive("u", 1)
     u_far[1] = (u_acc[before, part:] + u_in[1].astype(F32)).astype(BF16)
     send_u(u_far.at[1], 5, before)
+    give_w(2)
 
     z_device = z_first + core
     for a in (1, 0, 2):
@@ -556,29 +556,29 @@
 ):
     chips = n // 2
     quota = LANES // chips
-    rows_c = 4 * quota
-
-    def collect(k, base):
+    rows_d = 8 * quota
+
+    def collect(base):
         for half in range(2):
             for q in range(quota):
                 top = half * LANES + q * chips
                 for tb in range(2):
                     turned_ref[top : top + chips, tb * LANES : (tb + 1) * LANES] = stage[
-                        k, pl.ds(half * rows_c + base + q * 2 + tb, chips, stride=2 * rows_c), :
+                        pl.ds(half * rows_d + base + q * 2 + tb, chips, stride=2 * rows_d), :
                     ]
         return turned_ref[...].T
 
     stage[...] = b_back[...].reshape(stage.shape).astype(F32)
-    out_ref[...] = collect(0, 0).astype(BF16)
-    gf_ref[1] = collect(0, 2 * quota)
-    gf_ref[0] = collect(1, 0)
+    out_ref[...] = collect(0).astype(BF16)
+    gf_ref[1] = collect(2 * quota)
+    gf_ref[0] = collect(4 * quota)
     lane = lax.broadcasted_iota(jnp.int32, (1, LANES), 1)
     for f in range(2):
         for half in range(2):
             line = jnp.zeros((1, LANES), F32)
             for q in range(quota):
-                at = half * rows_c + 2 * quota + f * quota + q
-                row = jnp.sum(stage[1, pl.ds(at, chips, stride=2 * rows_c), :], axis=0, keepdims=True)
+                at = half * rows_d + 6 * quota + f * quota + q
+                row = jnp.sum(stage[pl.ds(at, chips, stride=2 * rows_d), :], axis=0, keepdims=True)
                 full = row + pltpu.roll(row, LANES - chips, 1) + pltpu.roll(row, LANES - 2 * chips, 1)
                 moved = full if q == 0 else pltpu.roll(full, q * chips, 1)
                 line = jnp.where((lane >= q * chips) & (lane < (q + 1) * chips), moved, line)
@@ -600,7 +600,7 @@
     plane = nx * ny
     quota = LANES // chips
     blocks = 4 * chips
-    rows_a, rows_b, rows_c = 12 * quota, 6 * quota, 4 * quota
+    rows_a, rows_b, rows_c, rows_d = 12 * quota, 6 * quota, 4 * quota, 8 * quota
     cols = 3 * LANES
     vmem = pl.BlockSpec(memory_space=pltpu.VMEM)
     smem = pl.BlockSpec(memory_space=pltpu.SMEM)
@@ -613,7 +613,7 @@
     landed = pl.pallas_call(
         functools.partial(layer_kernel, n, groups),
         out_shape=(
-            sds((2, n, rows_c, LANES), BF16),
+            sds((n, rows_d, LANES), BF16),
             sds((3, 2, rows, LANES), F32),
             sds((3, 2, rows, LANES), F32),
             sds((tokens, width), F32),
@@ -637,10 +637,10 @@
             pltpu.VMEM((n, rows_b, LANES), BF16),
             spec, spec, spec, spec, spec, spec,
             pltpu.VMEM((chips * rows_c, LANES), F32),
-            pltpu.VMEM((3, chips, rows_c, LANES), BF16),
-            pltpu.VMEM((3, chips, rows_c, LANES), BF16),
-            pltpu.VMEM((n * rows_c, LANES), F32),
-            pltpu.VMEM((2, n, rows_c, LANES), BF16),
+            pltpu.VMEM((chips, 3, rows_c, LANES), BF16),
+            pltpu.VMEM((chips, 3, rows_c, LANES), BF16),
+            pltpu.VMEM((n * rows_d, LANES), F32),
+            pltpu.VMEM((n, rows_d, LANES), BF16),
             pltpu.VMEM((LANES, 2 * tokens), F32),
             pltpu.VMEM((3, 2, tokens, LANES), BF16),
             pltpu.VMEM((3, tokens, LANES), BF16),
@@ -654,7 +654,7 @@
             dma((17,)),
             dma((2 * groups,)), dma((6,)), dma((2 * groups,)), dma((8,)), dma((6,)), dma((6,)),
             dma((3,)), dma((3,)), dma((3,)), dma((3,)),
-            dma((2,)), dma((2,)), dma((6,)), dma((6,)),
+            dma((6,)), dma((6,)),
         ],
         compiler_params=pltpu.CompilerParams(
             collective_id=0, has_side_effects=True, vmem_limit_bytes=limit
@@ -674,7 +674,7 @@
         in_specs=[vmem] * 4,
         out_specs=(vmem,) * 5,
         scratch_shapes=[
-            pltpu.VMEM((2, n * rows_c, LANES), F32),
+            pltpu.VMEM((n * rows_d, LANES), F32),
             pltpu.VMEM((2 * LANES, tokens), F32),
         ],
         compiler_params=pltpu.CompilerParams(vmem_limit_bytes=limit),

time: 68.4 us -> 73.2 us (1.070)
  Pallas kernels: 67.7 us -> 72.4 us
    pallas_call x1, Pallas kernels: 65.1 us -> 69.8 us  [on_device(): pl.pallas_call(functools.partial(layer_kernel, n, groups), out_shape=(sds...]
where the time goes in v5:
time: 73.2 us; the launch traced here: 73 us
  Pallas kernels  72.4 us (99%)
    pallas_call x1, Pallas kernels, on_device(): pl.pallas_call(functools.partial(layer_kernel, n, groups), out_shape=(sds...  69.8 us
    pallas_call x1, Pallas kernels, on_device(): pl.pallas_call(functools.partial(finish_kernel, n), out_shape=(sds((token...  2.64 us

profile of v5, /device:TPU:1, one launch (start us, length us, event | category | flops | bytes accessed | tf_op | source)
XLA Modules:
  0.0 73.0 jit_solution(5749789995944705040)
XLA Ops:
  0.6 69.8 %layer.1 = (bf16[64,32,128]{2,1,0:T(8,128)(2,1)}, f32[3,2,16,128]{3,2,1,0:T(8,128)}, f32[3,2,16,128]{3,2,1,0:T(8,128)}, f32[256,256]{1,0:T(8,128)}) custom-call(bf16[256,256]{1,0:T(8,128)(2,1)} %x_ref.1, bf16[3,16,256]{2,1,0:T(8,128)(2,1)} %bitcast.2, f32[2,256]{1,0:T(2,128)} %bias_ref.1, f32[2,256,256]{2,1,0:T(8,128)} %filters_at.1, ...), custom_call_target="tpu_custom_call" | custom-call | tf_op jit(solution)/shard_map/layer/pallas_call | solution.py:613
  70.4 2.6 %finish.1 = (bf16[256,256]{1,0:T(8,128)(2,1)}, bf16[256,256]{1,0:T(8,128)(2,1)}, f32[3,16,256]{2,1,0:T(8,128)}, f32[2,256,256]{2,1,0:T(8,128)}, f32[2,256]{1,0:T(2,128)}) custom-call(bf16[64,32,128]{2,1,0:T(8,128)(2,1)} %get-tuple-element.14.b_back, f32[3,2,16,128]{3,2,1,0:T(8,128)} %get-tuple-element.15.w_own, f32[3,2,16,128]{3,2,1,0:T(8,128)} %get-tuple-element.16.w_far, ...), custom_call_target="tpu_custom_call" | custom-call | tf_op jit(solution)/shard_map/finish/pallas_call | solution.py:665

commit v6 on v5

--- a/solution.py
+++ b/solution.py
@@ -112,6 +112,19 @@
     def in_plane(p, c, z):
         return (((p // ny) * 2 + z) * ny + lax.rem(p, ny)) * 2 + c
 
+    def hops(step, extent):
+        return min(step, extent - step)
+
+    moves = sorted(
+        ((dx, dz, dy) for dx in range(nx) for dz in range(2) for dy in range(ny)),
+        key=lambda move: -(hops(move[0], nx) + move[1] + hops(move[2], ny)),
+    )[:-1]
+
+    def moved(dx, dz, dy, c):
+        return (
+            (lax.rem(xx + dx, nx) * 2 + lax.rem(zl + dz, 2)) * ny + lax.rem(y + dy, ny)
+        ) * 2 + c
+
     pending = {}
 
     def expect(key, ref, sem):
@@ -175,13 +188,11 @@
     for k, (source, half) in enumerate(arrivals):
         expect(("x", k), half_x(core, source, half), x_sems.at[2 * source + half])
 
-    def send_w(step, carry):
-        peer = lax.rem(here + step, 2 * plane)
-        c = lax.rem(peer, 2)
-        send(w_ref.at[c], wg.at[me], sems.at[0], sems.at[1], in_plane(peer // 2, c, zl), group)
-        return carry
-
-    lax.fori_loop(1, 2 * plane, send_w, 0)
+    for dx, dz, dy in moves:
+        if dz == 0:
+            for c in range(2):
+                send(w_ref.at[c], wg.at[me], sems.at[0], sems.at[1], moved(dx, 0, dy, c), group)
+    send(w_ref.at[1 - core], wg.at[me], sems.at[0], sems.at[1], partner, group)
     pltpu.make_async_copy(w_ref.at[core], wg.at[me], sems.at[1]).start()
     expect(("w",), wg.at[pl.ds(0, 2 * plane)], sems.at[1])
     expect(("w out",), wg.at[pl.ds(0, 2 * plane + 1)], sems.at[0])
@@ -192,13 +203,10 @@
     spread(filters_ref[0], 0)
     wait_bytes(wg.at[pl.ds(z_first, 2)], sems.at[3])
 
-    def forward_w(step, carry):
-        p = lax.rem(here // 2 + step, plane)
-        pair = wg.at[pl.ds(z_first, 2)]
-        send(pair, pair, sems.at[4], sems.at[5], in_plane(p, core, zl), group)
-        return carry
-
-    lax.fori_loop(1, plane, forward_w, 0)
+    pair = wg.at[pl.ds(z_first, 2)]
+    for dx, dz, dy in moves:
+        if dz == 0:
+            send(pair, pair, sems.at[4], sems.at[5], moved(dx, 0, dy, core), group)
     expect(("w rest",), wg.at[pl.ds(0, 2 * plane - 2)], sems.at[5])
     expect(("w rest out",), wg.at[pl.ds(0, 2 * plane - 2)], sems.at[4])
     spread(filters_ref[1], 2 * quota)
@@ -219,15 +227,15 @@
         send(b_send.at[peer], b_recv.at[me], sems.at[9], sems.at[10], peer, group)
         return carry
 
-    lax.fori_loop(1, n, give_b, 0)
-    pltpu.make_async_copy(b_send.at[me], b_recv.at[me], sems.at[10]).start()
-    expect(("b",), b_recv, sems.at[10])
-    expect(("b out",), b_recv.at[pl.ds(0, n - 1)], sems.at[9])
     for k in (2, 3):
         arrive("x", k)
         relay_x(*arrivals[k], k)
     arrive("w")
     arrive("w rest")
+    lax.fori_loop(1, n, give_b, 0)
+    pltpu.make_async_copy(b_send.at[me], b_recv.at[me], sems.at[10]).start()
+    expect(("b",), b_recv, sems.at[10])
+    expect(("b out",), b_recv.at[pl.ds(0, n - 1)], sems.at[9])
 
     def weights(ref, c):
         return ref[pl.ds(c * slots, slots)].reshape(depth, cols)
@@ -269,12 +277,9 @@
     lay_out(1 - core)
     a_send[...] = stage_a[...].astype(BF16).reshape(a_send.shape)
 
-    def give_a(step, carry):
-        peer = lax.rem(chip + step, chips)
-        send(a_send.at[peer], a_recv.at[chip], sems.at[11], sems.at[12], 2 * peer + core, group)
-        return carry
-
-    lax.fori_loop(1, chips, give_a, 0)
+    for move in moves:
+        peer = moved(*move, core)
+        send(a_send.at[peer // 2], a_recv.at[chip], sems.at[11], sems.at[12], peer, group)
     pltpu.make_async_copy(a_send.at[chip], a_recv.at[chip], sems.at[12]).start()
     expect(("a",), a_recv, sems.at[12])
     expect(("a out",), a_recv.at[pl.ds(0, chips - 1)], sems.at[11])
@@ -357,12 +362,9 @@
         g_send[:, order[a]] = stage_c[...].astype(BF16).reshape(chips, rows_c, LANES)
 
     def give_late(k, span):
-        def one(step, carry):
-            peer = lax.rem(chip + step, chips)
-            send(g_send.at[peer, span], g_recv.at[chip, span], gs_sems.at[k], g_sems.at[k], 2 * peer + core, group)
-            return carry
-
-        lax.fori_loop(1, chips, one, 0)
+        for move in moves:
+            peer = moved(*move, core)
+            send(g_send.at[peer // 2, span], g_recv.at[chip, span], gs_sems.at[k], g_sems.at[k], peer, group)
         pltpu.make_async_copy(g_send.at[chip, span], g_recv.at[chip, span], g_sems.at[k]).start()
         expect(("g", k), g_recv.at[:, span], g_sems.at[k])
         expect(("g out", k), g_recv.at[pl.ds(0, chips - 1), span], gs_sems.at[k])
@@ -430,14 +432,14 @@
     grad_v = backward(spec_h1, spec_g1, True, False) + skip_one * grad_conv_one
     conv_two = backward(spec_h2, spec_z, False, False) + skip_two * mixed
     put_late(grad_v, 0)
+    give_late(1, pl.ds(1, 1))
     put_late(grad_out * conv_two, 2)
-    give_late(1, pl.ds(1, 2))
+    give_late(2, pl.ds(2, 1))
     put_early(gate_two * conv_two, 0)
     put_early(backward(spec_g2, spec_z, False, True), 2 * quota)
     put_early(backward(spec_g1, spec_v, False, True), 4 * quota)
     put_skip(grad_conv_one * values_v, 0)
     put_skip(grad_conv_two * mixed, 1)
-    give_early()
 
     def take(a):
         stage_c[...] = g_recv[:, order[a]].reshape(stage_c.shape).astype(F32)
@@ -482,6 +484,7 @@
 
     arrive("g", 0)
     take(1)
+    give_early()
     give_w(1)
     arrive("other")
     arrive("grad", 1)
@@ -489,7 +492,9 @@
         u_acc[c] = into_u(((1, True), (1, False)), c)
     arrive("g", 1)
     take(0)
+    arrive("g", 2)
     take(2)
+    give_w(0)
     for c in range(groups):
         u_acc[c] = u_acc[c] + into_u(((0, True), (2, True)), c)
     arrive("grad", 0)
@@ -518,15 +523,14 @@
     send_u(half_u(after, 1), 2, after)
     finish_u(before)
     send_u(half_u(before, 0), 3, before)
+    give_w(2)
     u_own[...] = u_acc[group] + into_last(group)
-    give_w(0)
     arrive("u", 0)
     u_far[0] = (u_acc[after, :part] + u_in[0].astype(F32)).astype(BF16)
     send_u(u_far.at[0], 4, after)
     arrive("u", 1)
     u_far[1] = (u_acc[before, part:] + u_in[1].astype(F32)).astype(BF16)
     send_u(u_far.at[1], 5, before)
-    give_w(2)
 
     z_device = z_first + core
     for a in (1, 0, 2):

time: 73.2 us -> 66.5 us (0.908)
  Pallas kernels: 72.4 us -> 65.7 us
    pallas_call x1, Pallas kernels: 69.8 us -> 63.1 us  [on_device(): pl.pallas_call(functools.partial(layer_kernel, n, groups), out_shape=(sds...]
where the time goes in v6:
time: 66.5 us; the launch traced here: 66.4 us
  Pallas kernels  65.7 us (99%)
    pallas_call x1, Pallas kernels, on_device(): pl.pallas_call(functools.partial(layer_kernel, n, groups), out_shape=(sds...  63.1 us
    pallas_call x1, Pallas kernels, on_device(): pl.pallas_call(functools.partial(finish_kernel, n), out_shape=(sds((token...  2.64 us

profile of v6, /device:TPU:1, one launch (start us, length us, event | category | flops | bytes accessed | tf_op | source)
XLA Modules:
  0.0 66.4 jit_solution(11694004801783926293)
XLA Ops:
  0.6 63.1 %layer.1 = (bf16[64,32,128]{2,1,0:T(8,128)(2,1)}, f32[3,2,16,128]{3,2,1,0:T(8,128)}, f32[3,2,16,128]{3,2,1,0:T(8,128)}, f32[256,256]{1,0:T(8,128)}) custom-call(bf16[256,256]{1,0:T(8,128)(2,1)} %x_ref.1, bf16[3,16,256]{2,1,0:T(8,128)(2,1)} %bitcast.2, f32[2,256]{1,0:T(2,128)} %bias_ref.1, f32[2,256,256]{2,1,0:T(8,128)} %filters_at.1, ...), custom_call_target="tpu_custom_call" | custom-call | tf_op jit(solution)/shard_map/layer/pallas_call | solution.py:617
  63.7 2.6 %finish.1 = (bf16[256,256]{1,0:T(8,128)(2,1)}, bf16[256,256]{1,0:T(8,128)(2,1)}, f32[3,16,256]{2,1,0:T(8,128)}, f32[2,256,256]{2,1,0:T(8,128)}, f32[2,256]{1,0:T(2,128)}) custom-call(bf16[64,32,128]{2,1,0:T(8,128)(2,1)} %get-tuple-element.14.b_back, f32[3,2,16,128]{3,2,1,0:T(8,128)} %get-tuple-element.15.w_own, f32[3,2,16,128]{3,2,1,0:T(8,128)} %get-tuple-element.16.w_far, ...), custom_call_target="tpu_custom_call" | custom-call | tf_op jit(solution)/shard_map/finish/pallas_call | solution.py:669

commit v7 on v6

--- a/solution.py
+++ b/solution.py
@@ -461,19 +461,31 @@
                 s = c * slots + k
                 w_send[a, s // (4 * ny), (s // (2 * ny)) % 2, s % (2 * ny)] = term[k]
 
-        def one(step, carry):
-            peer = lax.rem(here + step, 2 * plane)
-            p, c = peer // 2, lax.rem(peer, 2)
-            send(
-                w_send.at[a, p // ny, :, lax.rem(p, ny) * 2 + c], w_in.at[a, here],
-                ws_sems.at[a], w_sems.at[a], in_plane(p, c, zl), group,
-            )
-            return carry
-
-        lax.fori_loop(1, 2 * plane, one, 0)
+        for dx, dz, dy in moves + [(0, 0, 0)]:
+            for c in range(2) if dx + dy else ([1 - core] if dz == 0 else []):
+                if dz == 0:
+                    px, py = lax.rem(xx + dx, nx), lax.rem(y + dy, ny)
+                    send(
+                        w_send.at[a, px, :, py * 2 + c], w_in.at[a, here],
+                        ws_sems.at[a], w_sems.at[a], moved(dx, 0, dy, c), group,
+                    )
         pltpu.make_async_copy(w_send.at[a, xx, :, y * 2 + core], w_in.at[a, here], w_sems.at[a]).start()
         expect(("sum", a), w_in.at[a], w_sems.at[a])
         expect(("sum out", a), w_in.at[a, pl.ds(0, 2 * plane - 1)], ws_sems.at[a])
+
+    def relay_w(a):
+        arrive("sum", a)
+        for half in range(2):
+            own = w_in[a, half, zl].astype(F32)
+            away = w_in[a, half, 1 - zl].astype(F32)
+            for p in range(1, plane):
+                own = own + w_in[a, 2 * p + half, zl].astype(F32)
+                away = away + w_in[a, 2 * p + half, 1 - zl].astype(F32)
+            w_own[a, half] = own
+            w_relay[a, half] = away
+        send(w_relay.at[a], w_far.at[a], ws_sems.at[3 + a], w_sems.at[3 + a], z_first + core, group)
+        expect(("far", a), w_far.at[a], w_sems.at[3 + a])
+        expect(("far out", a), w_far.at[a], ws_sems.at[3 + a])
 
     def into_u(terms, c):
         left, right = [], []
@@ -525,6 +537,7 @@
     send_u(half_u(before, 0), 3, before)
     give_w(2)
     u_own[...] = u_acc[group] + into_last(group)
+    relay_w(1)
     arrive("u", 0)
     u_far[0] = (u_acc[after, :part] + u_in[0].astype(F32)).astype(BF16)
     send_u(u_far.at[0], 4, after)
@@ -532,20 +545,8 @@
     u_far[1] = (u_acc[before, part:] + u_in[1].astype(F32)).astype(BF16)
     send_u(u_far.at[1], 5, before)
 
-    z_device = z_first + core
-    for a in (1, 0, 2):
-        arrive("sum", a)
-        for half in range(2):
-            own = w_in[a, half, zl].astype(F32)
-            away = w_in[a, half, 1 - zl].astype(F32)
-            for p in range(1, plane):
-                own = own + w_in[a, 2 * p + half, zl].astype(F32)
-                away = away + w_in[a, 2 * p + half, 1 - zl].astype(F32)
-            w_own[a, half] = own
-            w_relay[a, half] = away
-        send(w_relay.at[a], w_far.at[a], ws_sems.at[3 + a], w_sems.at[3 + a], z_device, group)
-        expect(("far", a), w_far.at[a], w_sems.at[3 + a])
-        expect(("far out", a), w_far.at[a], ws_sems.at[3 + a])
+    relay_w(0)
+    relay_w(2)
 
     for slot in range(2, 6):
         arrive("u", slot)

time: 66.5 us -> 67.3 us (1.012); the launches traced: 66.4 us -> 66.1 us
  no operation moved by 1% of the time
where the time goes in v7:
time: 67.3 us; the launch traced here: 66.1 us
  Pallas kernels  65.5 us (97%)
    pallas_call x1, Pallas kernels, on_device(): pl.pallas_call(functools.partial(layer_kernel, n, groups), out_shape=(sds...  62.8 us
    pallas_call x1, Pallas kernels, on_device(): pl.pallas_call(functools.partial(finish_kernel, n), out_shape=(sds((token...  2.64 us

profile of v7, /device:TPU:1, one launch (start us, length us, event | category | flops | bytes accessed | tf_op | source)
XLA Modules:
  0.0 66.1 jit_solution(18341798515986486144)
XLA Ops:
  0.6 62.8 %layer.1 = (bf16[64,32,128]{2,1,0:T(8,128)(2,1)}, f32[3,2,16,128]{3,2,1,0:T(8,128)}, f32[3,2,16,128]{3,2,1,0:T(8,128)}, f32[256,256]{1,0:T(8,128)}) custom-call(bf16[256,256]{1,0:T(8,128)(2,1)} %x_ref.1, bf16[3,16,256]{2,1,0:T(8,128)(2,1)} %bitcast.2, f32[2,256]{1,0:T(2,128)} %bias_ref.1, f32[2,256,256]{2,1,0:T(8,128)} %filters_at.1, ...), custom_call_target="tpu_custom_call" | custom-call | tf_op jit(solution)/shard_map/layer/pallas_call | solution.py:618
  63.5 2.6 %finish.1 = (bf16[256,256]{1,0:T(8,128)(2,1)}, bf16[256,256]{1,0:T(8,128)(2,1)}, f32[3,16,256]{2,1,0:T(8,128)}, f32[2,256,256]{2,1,0:T(8,128)}, f32[2,256]{1,0:T(2,128)}) custom-call(bf16[64,32,128]{2,1,0:T(8,128)(2,1)} %get-tuple-element.14.b_back, f32[3,2,16,128]{3,2,1,0:T(8,128)} %get-tuple-element.15.w_own, f32[3,2,16,128]{3,2,1,0:T(8,128)} %get-tuple-element.16.w_far, ...), custom_call_target="tpu_custom_call" | custom-call | tf_op jit(solution)/shard_map/finish/pallas_call | solution.py:670
